TPU v7x, 32 devices: a whole 2x2x4 slice. The times are simulated.
32 devices in a mesh: gx: 4 (over z), gy: 4 (over y, x), gz: 2 (over core).
Axes of the slice: x: 2, y: 2, z: 4, core: 2. Of those that a mesh axis runs over, the one named last changes fastest.
Arguments:
- features: bfloat16 [8, 16, 2, 128, 256], P('gx', 'gy', 'gz'), may hold values from -6 to 6
- fractions: bfloat16 [8, 16, 2, 3, 128], P('gx', 'gy', 'gz'), may hold values from 0 to 0.98828125
- occupied: int32 [8, 16, 2, 128], P('gx', 'gy', 'gz'), may hold values 0 or 1
- wave_index: int32 [3, 512], replicated, may hold values from -14 to 14, as said below
- radial_weight: float32 [8, 4], replicated, may hold values from -4 to 4
- ewald_mix: float32 [256, 256], replicated, may hold values from -0.375 to 0.375
- msg_weight: bfloat16 [256, 256], replicated, may hold values from -0.375 to 0.375
- ewald_weight: bfloat16 [256, 256], replicated, may hold values from -0.375 to 0.375
- out_weight: bfloat16 [256, 256], replicated, may hold values from -0.375 to 0.375
Outputs:
- updated: bfloat16 [8, 16, 2, 128, 256], P('gx', 'gy', 'gz')
Inputs may be any that keep to these rules, and one draw needn't show every extreme that they name: `wave_index`: no wavevector is zero, and no two wavevectors are equal or opposite.
All inputs are finite; a program needn't handle non-finite values. No bound on the sum of `occupied` on one device may be relied on, other than what follows from the above.
Results may differ from a plain program's by a relative error of at most 0.007.
Values may be sent and summed in bfloat16 or wider, within the bound.
A program may use at most 64 MiB of HBM per device.

v0:
```python
import math

import jax
import jax.numpy as jnp
from jax import lax
from jax.sharding import PartitionSpec as P

sharpness = 16.0
smearing = 0.04
screening = 4.0
strength = 24.0


def padded(x, sides, width):
    for axis, dim in sides:
        count, length = (lax.axis_size(axis), x.shape[dim])
        up = [(i, (i + 1) % count) for i in range(count)]
        down = [(j, i) for i, j in up]
        last = lax.slice_in_dim(x, length - width, length, axis=dim)
        first = lax.slice_in_dim(x, 0, width, axis=dim)
        before = lax.ppermute(last, axis, up)
        after = lax.ppermute(first, axis, down)
        x = jnp.concatenate([before, x, after], axis=dim)
    return x


def pair_weights(home_geom, near_geom, shift_vec, radial_weight, self_pair):
    slot_count = home_geom.shape[2]
    dist_sq = jnp.zeros((home_geom.shape[0], slot_count, slot_count), jnp.float32)
    for axis_id in range(3):
        axis_gap = (
            near_geom[:, axis_id, None, :] + shift_vec[axis_id] - home_geom[:, axis_id, :, None]
        )
        dist_sq = dist_sq + axis_gap * axis_gap
    distance = jnp.sqrt(dist_sq)
    envelope = jnp.square(jnp.maximum(1.0 - dist_sq, 0.0)) * near_geom[:, 3, None, :]
    envelope = envelope * (1.0 - self_pair * jnp.eye(slot_count, dtype=jnp.float32))
    level_count = radial_weight.shape[0]
    radial_sum = jnp.zeros(
        (home_geom.shape[0], radial_weight.shape[1], slot_count, slot_count), jnp.float32
    )
    for level_id in range(level_count):
        radial_bump = jnp.exp(-sharpness * jnp.square(distance - level_id / (level_count - 1)))
        radial_sum = (
            radial_sum + radial_bump[:, None] * radial_weight[level_id][None, :, None, None]
        )
    return (radial_sum * envelope[:, None]).astype(jnp.bfloat16)


def body(
    features,
    fractions,
    occupied,
    wave_index,
    radial_weight,
    ewald_mix,
    msg_weight,
    ewald_weight,
    out_weight,
):
    cells_x, cells_y, cells_z, slot_count, feat_width = features.shape
    head_count = radial_weight.shape[1]
    head_width = feat_width // head_count
    cell_count = cells_x * cells_y * cells_z
    atom_rows = cell_count * slot_count
    geometry = jnp.concatenate([fractions, occupied[:, :, :, None, :].astype(jnp.bfloat16)], axis=3)
    wide_feat = padded(features, (("gx", 0), ("gy", 1), ("gz", 2)), 1)
    wide_geom = padded(geometry, (("gx", 0), ("gy", 1), ("gz", 2)), 1)
    home_geom = geometry.reshape(cell_count, 4, slot_count).astype(jnp.float32)
    anchor = jnp.int32(0)

    def add_offset(offset_id, msg_sum):
        step_x = offset_id // 9 - 1
        step_y = offset_id // 3 % 3 - 1
        step_z = offset_id % 3 - 1
        near_feat = lax.dynamic_slice(
            wide_feat,
            (step_x + 1, step_y + 1, step_z + 1, anchor, anchor),
            (cells_x, cells_y, cells_z, slot_count, feat_width),
        )
        near_feat = near_feat.reshape(cell_count, slot_count, head_count, head_width)
        near_geom = lax.dynamic_slice(
            wide_geom,
            (step_x + 1, step_y + 1, step_z + 1, anchor, anchor),
            (cells_x, cells_y, cells_z, 4, slot_count),
        )
        near_geom = near_geom.reshape(cell_count, 4, slot_count).astype(jnp.float32)
        shift_vec = jnp.stack([step_x, step_y, step_z]).astype(jnp.float32)
        self_pair = (offset_id == 13).astype(jnp.float32)
        weights = pair_weights(home_geom, near_geom, shift_vec, radial_weight, self_pair)
        return msg_sum + jnp.einsum(
            "nhpq,nqhc->nphc", weights, near_feat, preferred_element_type=jnp.float32
        )

    msg_sum = lax.fori_loop(
        0, 27, add_offset, jnp.zeros((cell_count, slot_count, head_count, head_width), jnp.float32)
    )
    scaled = msg_sum.reshape(cell_count, slot_count, feat_width) * (
        1.0 / math.sqrt(4.0 * slot_count)
    )
    messages = scaled.astype(jnp.bfloat16).reshape(atom_rows, feat_width)
    grid_x = lax.axis_size("gx") * cells_x
    grid_y = lax.axis_size("gy") * cells_y
    grid_z = lax.axis_size("gz") * cells_z
    devices = lax.axis_size("gx") * lax.axis_size("gy") * lax.axis_size("gz")
    wave_count = wave_index.shape[1]
    lengths = jnp.array([grid_x, grid_y, grid_z], jnp.float32)
    wave_vec = 2.0 * math.pi * wave_index.astype(jnp.float32) / lengths[:, None]
    wave_sq = jnp.sum(wave_vec * wave_vec, axis=0)
    damping = (
        strength
        * jnp.exp(-0.5 * smearing * wave_sq)
        / (wave_sq + screening)
        * (1.0 / math.sqrt(atom_rows * devices * wave_count))
    )
    start_x = (lax.axis_index("gx") * cells_x + jnp.arange(cells_x, dtype=jnp.int32)).astype(
        jnp.float32
    )[:, None, None, None]
    start_y = (lax.axis_index("gy") * cells_y + jnp.arange(cells_y, dtype=jnp.int32)).astype(
        jnp.float32
    )[None, :, None, None]
    start_z = (lax.axis_index("gz") * cells_z + jnp.arange(cells_z, dtype=jnp.int32)).astype(
        jnp.float32
    )[None, None, :, None]
    local_frac = fractions.astype(jnp.float32)
    pos_x = start_x + local_frac[:, :, :, 0]
    pos_y = start_y + local_frac[:, :, :, 1]
    pos_z = start_z + local_frac[:, :, :, 2]
    phase_rows = (
        pos_x[..., None] * wave_vec[0]
        + pos_y[..., None] * wave_vec[1]
        + pos_z[..., None] * wave_vec[2]
    )
    phase_rows = phase_rows.reshape(atom_rows, wave_count)
    wave_basis = jnp.concatenate([jnp.cos(phase_rows), jnp.sin(phase_rows)], axis=1).astype(
        jnp.bfloat16
    )
    masked = (features * occupied[..., None].astype(jnp.bfloat16)).reshape(atom_rows, feat_width)
    partial_value = lax.dot_general(
        wave_basis, masked, (((0,), (0,)), ((), ())), preferred_element_type=jnp.float32
    )
    partial_value = partial_value.reshape(2, wave_count, feat_width)
    wave_share = lax.psum_scatter(
        partial_value, ("gx", "gy", "gz"), scatter_dimension=1, tiled=True
    )
    share_rows = wave_share.shape[1]
    share_start = lax.axis_index(("gx", "gy", "gz")) * share_rows
    share_damp = lax.dynamic_slice_in_dim(damping, share_start, share_rows, 0)
    mixed_rows = jnp.dot(
        wave_share.reshape(2 * share_rows, feat_width), ewald_mix, precision=lax.Precision.HIGHEST
    )
    mixed_rows = mixed_rows.reshape(2, share_rows, feat_width)
    filtered = lax.all_gather(
        (mixed_rows * share_damp[None, :, None]).astype(jnp.bfloat16),
        ("gx", "gy", "gz"),
        axis=1,
        tiled=True,
    )
    values = jnp.dot(
        wave_basis, filtered.reshape(2 * wave_count, feat_width), preferred_element_type=jnp.float32
    )
    ewald_out = values.astype(jnp.bfloat16)
    joined = jnp.dot(messages, msg_weight, preferred_element_type=jnp.float32) + jnp.dot(
        ewald_out, ewald_weight, preferred_element_type=jnp.float32
    )
    hidden = jax.nn.silu(joined).astype(jnp.bfloat16)
    result = features.reshape(atom_rows, feat_width).astype(jnp.float32) + jnp.dot(
        hidden, out_weight, preferred_element_type=jnp.float32
    )
    result = result * occupied.reshape(atom_rows, 1).astype(jnp.float32)
    return result.astype(jnp.bfloat16).reshape(features.shape)


def solution(mesh):
    in_specs = (
        P("gx", "gy", "gz", None, None),
        P("gx", "gy", "gz", None, None),
        P("gx", "gy", "gz", None),
        P(),
        P(),
        P(),
        P(),
        P(),
        P(),
    )
    out_specs = P("gx", "gy", "gz", None, None)
    return jax.shard_map(body, mesh=mesh, in_specs=in_specs, out_specs=out_specs, check_vma=False)
```

profile of v0, /device:TPU:0, one launch (start us, length us, event | category | flops | bytes accessed | tf_op | source)
XLA Modules:
  0.0 411.5 jit_solution(6668553915599535012)
XLA Ops:
  18.8 8.9 %cosine_convert_fusion = (bf16[1024,512]{1,0:T(8,128)(2,1)S(1)}, bf16[1024,512]{1,0:T(8,128)(2,1)S(1)}) fusion(f32[512]{0:T(512)S(1)} %bitcast.132, f32[1024]{0:T(1024)S(1)} %bitcast.126, f32[512]{0:T(512)S(1)} %bitcast.133, f32[1024]{0:T(1024)S(1)} %add.812, f32[512]{0:T(512)S(1)} %bitcast.131, f32[1024]{0:T(1024)S(1)} %add.807), kind=kLoop, calls=%fused_computation.57 | loop fusion | flops 3670016 | bytes 2115584 | tf_op jit(solution)/shard_map/convert.2
  32.1 6.1 %collective-permute-done.2 = bf16[4,1,1,128,256]{3,4,1,0,2:T(8,128)(2,1)S(1)} collective-permute-done((bf16[4,1,1,128,256]{3,4,1,0,2:T(8,128)(2,1)S(1)}, bf16[4,1,1,128,256]{3,4,1,0,2:T(8,128)(2,1)S(1)}, u32[]{:S(2)}, u32[]{:S(2)}) %collective-permute-start.2) | collective-permute-done | bytes 262176 | tf_op jit(solution)/shard_map/ppermute | solution.py:21
  57.6 5.1 %pad_maximum_fusion = bf16[4,6,3,128,256]{3,4,1,0,2:T(8,128)(2,1)} fusion(bf16[4,6,1,128,256]{3,4,1,0,2:T(8,128)(2,1)} %collective-permute-done.5, bf16[4,1,1,128,256]{3,4,1,0,2:T(8,128)(2,1)} %copy-done.8, bf16[1,4,1,128,256]{3,4,1,0,2:T(8,128)(2,1)S(1)} %collective-permute-done.1, bf16[2,4,1,128,256]{3,4,1,0,2:T(8,128)(2,1)S(1)} %copy.19, ...), kind=kLoop, calls=%fused_computation.54 | loop fusion | flops 14155776 | bytes 9437184 | tf_op jit(solution)/shard_map/concatenate | solution.py:23
  62.7 290.6 %while.19 = (s32[]{:T(128)}, f32[8,128,4,64]{1,3,2,0:T(8,128)}, bf16[4,6,3,128,256]{3,4,1,0,2:T(8,128)(2,1)}, bf16[4,6,3,4,128]{4,1,0,3,2:T(8,128)(2,1)S(1)}, f3...) while((s32[]{:T(128)}, f32[8,128,4,64]{1,3,2,0:T(8,128)}, ...), condition=%wide.region_1.2_spmd.clone, body=%wide.region_0.1_spmd.clone.sunk | while | flops 81321008 | bytes 13366249 | solution.py:95
  69.2 4.0 fusion.62
  79.6 4.4 %fusion.62 = f32[8,128,4,64]{1,3,2,0:T(8,128)} fusion(bf16[8,128,4,64]{1,3,2,0:T(8,128)(2,1)S(1)} %bitcast.114, f32[8,128,4,64]{1,3,2,0:T(8,128)} %get-tuple-element.477, f32[8,128,128]{2,1,0:T(8,128)S(1)} %get-tuple-element.445, f32[4]{0:T(128)S(1)} %get-tuple-element.446, f32[8,128,128]{2,1,0:T(8,128)S(1)} %get-tuple-element.447, ...), kind=kOutput, calls=%fused_computation.2.clone.1 | convolution fusion | flops 76546048 | bytes 7340161 | tf_op jit(solution)/shard_map/while/body/eval_jaxpr/nhpq,nqhc->nphc/dot_general | solution.py:91
  90.4 4.4 %fusion.62 = f32[8,128,4,64]{1,3,2,0:T(8,128)} fusion(bf16[8,128,4,64]{1,3,2,0:T(8,128)(2,1)S(1)} %bitcast.114, f32[8,128,4,64]{1,3,2,0:T(8,128)} %get-tuple-element.477, f32[8,128,128]{2,1,0:T(8,128)S(1)} %get-tuple-element.445, f32[4]{0:T(128)S(1)} %get-tuple-element.446, f32[8,128,128]{2,1,0:T(8,128)S(1)} %get-tuple-element.447, ...), kind=kOutput, calls=%fused_computation.2.clone.1 | convolution fusion | flops 76546048 | bytes 7340161 | tf_op jit(solution)/shard_map/while/body/eval_jaxpr/nhpq,nqhc->nphc/dot_general | solution.py:91
  101.1 4.4 %fusion.62 = f32[8,128,4,64]{1,3,2,0:T(8,128)} fusion(bf16[8,128,4,64]{1,3,2,0:T(8,128)(2,1)S(1)} %bitcast.114, f32[8,128,4,64]{1,3,2,0:T(8,128)} %get-tuple-element.477, f32[8,128,128]{2,1,0:T(8,128)S(1)} %get-tuple-element.445, f32[4]{0:T(128)S(1)} %get-tuple-element.446, f32[8,128,128]{2,1,0:T(8,128)S(1)} %get-tuple-element.447, ...), kind=kOutput, calls=%fused_computation.2.clone.1 | convolution fusion | flops 76546048 | bytes 7340161 | tf_op jit(solution)/shard_map/while/body/eval_jaxpr/nhpq,nqhc->nphc/dot_general | solution.py:91
  111.9 4.4 %fusion.62 = f32[8,128,4,64]{1,3,2,0:T(8,128)} fusion(bf16[8,128,4,64]{1,3,2,0:T(8,128)(2,1)S(1)} %bitcast.114, f32[8,128,4,64]{1,3,2,0:T(8,128)} %get-tuple-element.477, f32[8,128,128]{2,1,0:T(8,128)S(1)} %get-tuple-element.445, f32[4]{0:T(128)S(1)} %get-tuple-element.446, f32[8,128,128]{2,1,0:T(8,128)S(1)} %get-tuple-element.447, ...), kind=kOutput, calls=%fused_computation.2.clone.1 | convolution fusion | flops 76546048 | bytes 7340161 | tf_op jit(solution)/shard_map/while/body/eval_jaxpr/nhpq,nqhc->nphc/dot_general | solution.py:91
  122.7 4.4 %fusion.62 = f32[8,128,4,64]{1,3,2,0:T(8,128)} fusion(bf16[8,128,4,64]{1,3,2,0:T(8,128)(2,1)S(1)} %bitcast.114, f32[8,128,4,64]{1,3,2,0:T(8,128)} %get-tuple-element.477, f32[8,128,128]{2,1,0:T(8,128)S(1)} %get-tuple-element.445, f32[4]{0:T(128)S(1)} %get-tuple-element.446, f32[8,128,128]{2,1,0:T(8,128)S(1)} %get-tuple-element.447, ...), kind=kOutput, calls=%fused_computation.2.clone.1 | convolution fusion | flops 76546048 | bytes 7340161 | tf_op jit(solution)/shard_map/while/body/eval_jaxpr/nhpq,nqhc->nphc/dot_general | solution.py:91
  133.5 4.4 %fusion.62 = f32[8,128,4,64]{1,3,2,0:T(8,128)} fusion(bf16[8,128,4,64]{1,3,2,0:T(8,128)(2,1)S(1)} %bitcast.114, f32[8,128,4,64]{1,3,2,0:T(8,128)} %get-tuple-element.477, f32[8,128,128]{2,1,0:T(8,128)S(1)} %get-tuple-element.445, f32[4]{0:T(128)S(1)} %get-tuple-element.446, f32[8,128,128]{2,1,0:T(8,128)S(1)} %get-tuple-element.447, ...), kind=kOutput, calls=%fused_computation.2.clone.1 | convolution fusion | flops 76546048 | bytes 7340161 | tf_op jit(solution)/shard_map/while/body/eval_jaxpr/nhpq,nqhc->nphc/dot_general | solution.py:91
  144.3 4.4 %fusion.62 = f32[8,128,4,64]{1,3,2,0:T(8,128)} fusion(bf16[8,128,4,64]{1,3,2,0:T(8,128)(2,1)S(1)} %bitcast.114, f32[8,128,4,64]{1,3,2,0:T(8,128)} %get-tuple-element.477, f32[8,128,128]{2,1,0:T(8,128)S(1)} %get-tuple-element.445, f32[4]{0:T(128)S(1)} %get-tuple-element.446, f32[8,128,128]{2,1,0:T(8,128)S(1)} %get-tuple-element.447, ...), kind=kOutput, calls=%fused_computation.2.clone.1 | convolution fusion | flops 76546048 | bytes 7340161 | tf_op jit(solution)/shard_map/while/body/eval_jaxpr/nhpq,nqhc->nphc/dot_general | solution.py:91
  155.0 4.4 %fusion.62 = f32[8,128,4,64]{1,3,2,0:T(8,128)} fusion(bf16[8,128,4,64]{1,3,2,0:T(8,128)(2,1)S(1)} %bitcast.114, f32[8,128,4,64]{1,3,2,0:T(8,128)} %get-tuple-element.477, f32[8,128,128]{2,1,0:T(8,128)S(1)} %get-tuple-element.445, f32[4]{0:T(128)S(1)} %get-tuple-element.446, f32[8,128,128]{2,1,0:T(8,128)S(1)} %get-tuple-element.447, ...), kind=kOutput, calls=%fused_computation.2.clone.1 | convolution fusion | flops 76546048 | bytes 7340161 | tf_op jit(solution)/shard_map/while/body/eval_jaxpr/nhpq,nqhc->nphc/dot_general | solution.py:91
  165.8 4.4 %fusion.62 = f32[8,128,4,64]{1,3,2,0:T(8,128)} fusion(bf16[8,128,4,64]{1,3,2,0:T(8,128)(2,1)S(1)} %bitcast.114, f32[8,128,4,64]{1,3,2,0:T(8,128)} %get-tuple-element.477, f32[8,128,128]{2,1,0:T(8,128)S(1)} %get-tuple-element.445, f32[4]{0:T(128)S(1)} %get-tuple-element.446, f32[8,128,128]{2,1,0:T(8,128)S(1)} %get-tuple-element.447, ...), kind=kOutput, calls=%fused_computation.2.clone.1 | convolution fusion | flops 76546048 | bytes 7340161 | tf_op jit(solution)/shard_map/while/body/eval_jaxpr/nhpq,nqhc->nphc/dot_general | solution.py:91
  176.6 4.4 %fusion.62 = f32[8,128,4,64]{1,3,2,0:T(8,128)} fusion(bf16[8,128,4,64]{1,3,2,0:T(8,128)(2,1)S(1)} %bitcast.114, f32[8,128,4,64]{1,3,2,0:T(8,128)} %get-tuple-element.477, f32[8,128,128]{2,1,0:T(8,128)S(1)} %get-tuple-element.445, f32[4]{0:T(128)S(1)} %get-tuple-element.446, f32[8,128,128]{2,1,0:T(8,128)S(1)} %get-tuple-element.447, ...), kind=kOutput, calls=%fused_computation.2.clone.1 | convolution fusion | flops 76546048 | bytes 7340161 | tf_op jit(solution)/shard_map/while/body/eval_jaxpr/nhpq,nqhc->nphc/dot_general | solution.py:91
  187.4 4.4 %fusion.62 = f32[8,128,4,64]{1,3,2,0:T(8,128)} fusion(bf16[8,128,4,64]{1,3,2,0:T(8,128)(2,1)S(1)} %bitcast.114, f32[8,128,4,64]{1,3,2,0:T(8,128)} %get-tuple-element.477, f32[8,128,128]{2,1,0:T(8,128)S(1)} %get-tuple-element.445, f32[4]{0:T(128)S(1)} %get-tuple-element.446, f32[8,128,128]{2,1,0:T(8,128)S(1)} %get-tuple-element.447, ...), kind=kOutput, calls=%fused_computation.2.clone.1 | convolution fusion | flops 76546048 | bytes 7340161 | tf_op jit(solution)/shard_map/while/body/eval_jaxpr/nhpq,nqhc->nphc/dot_general | solution.py:91
  198.2 4.4 %fusion.62 = f32[8,128,4,64]{1,3,2,0:T(8,128)} fusion(bf16[8,128,4,64]{1,3,2,0:T(8,128)(2,1)S(1)} %bitcast.114, f32[8,128,4,64]{1,3,2,0:T(8,128)} %get-tuple-element.477, f32[8,128,128]{2,1,0:T(8,128)S(1)} %get-tuple-element.445, f32[4]{0:T(128)S(1)} %get-tuple-element.446, f32[8,128,128]{2,1,0:T(8,128)S(1)} %get-tuple-element.447, ...), kind=kOutput, calls=%fused_computation.2.clone.1 | convolution fusion | flops 76546048 | bytes 7340161 | tf_op jit(solution)/shard_map/while/body/eval_jaxpr/nhpq,nqhc->nphc/dot_general | solution.py:91
  208.9 4.4 %fusion.62 = f32[8,128,4,64]{1,3,2,0:T(8,128)} fusion(bf16[8,128,4,64]{1,3,2,0:T(8,128)(2,1)S(1)} %bitcast.114, f32[8,128,4,64]{1,3,2,0:T(8,128)} %get-tuple-element.477, f32[8,128,128]{2,1,0:T(8,128)S(1)} %get-tuple-element.445, f32[4]{0:T(128)S(1)} %get-tuple-element.446, f32[8,128,128]{2,1,0:T(8,128)S(1)} %get-tuple-element.447, ...), kind=kOutput, calls=%fused_computation.2.clone.1 | convolution fusion | flops 76546048 | bytes 7340161 | tf_op jit(solution)/shard_map/while/body/eval_jaxpr/nhpq,nqhc->nphc/dot_general | solution.py:91
  219.7 4.4 %fusion.62 = f32[8,128,4,64]{1,3,2,0:T(8,128)} fusion(bf16[8,128,4,64]{1,3,2,0:T(8,128)(2,1)S(1)} %bitcast.114, f32[8,128,4,64]{1,3,2,0:T(8,128)} %get-tuple-element.477, f32[8,128,128]{2,1,0:T(8,128)S(1)} %get-tuple-element.445, f32[4]{0:T(128)S(1)} %get-tuple-element.446, f32[8,128,128]{2,1,0:T(8,128)S(1)} %get-tuple-element.447, ...), kind=kOutput, calls=%fused_computation.2.clone.1 | convolution fusion | flops 76546048 | bytes 7340161 | tf_op jit(solution)/shard_map/while/body/eval_jaxpr/nhpq,nqhc->nphc/dot_general | solution.py:91
  230.5 4.4 %fusion.62 = f32[8,128,4,64]{1,3,2,0:T(8,128)} fusion(bf16[8,128,4,64]{1,3,2,0:T(8,128)(2,1)S(1)} %bitcast.114, f32[8,128,4,64]{1,3,2,0:T(8,128)} %get-tuple-element.477, f32[8,128,128]{2,1,0:T(8,128)S(1)} %get-tuple-element.445, f32[4]{0:T(128)S(1)} %get-tuple-element.446, f32[8,128,128]{2,1,0:T(8,128)S(1)} %get-tuple-element.447, ...), kind=kOutput, calls=%fused_computation.2.clone.1 | convolution fusion | flops 76546048 | bytes 7340161 | tf_op jit(solution)/shard_map/while/body/eval_jaxpr/nhpq,nqhc->nphc/dot_general | solution.py:91
  241.2 4.4 %fusion.62 = f32[8,128,4,64]{1,3,2,0:T(8,128)} fusion(bf16[8,128,4,64]{1,3,2,0:T(8,128)(2,1)S(1)} %bitcast.114, f32[8,128,4,64]{1,3,2,0:T(8,128)} %get-tuple-element.477, f32[8,128,128]{2,1,0:T(8,128)S(1)} %get-tuple-element.445, f32[4]{0:T(128)S(1)} %get-tuple-element.446, f32[8,128,128]{2,1,0:T(8,128)S(1)} %get-tuple-element.447, ...), kind=kOutput, calls=%fused_computation.2.clone.1 | convolution fusion | flops 76546048 | bytes 7340161 | tf_op jit(solution)/shard_map/while/body/eval_jaxpr/nhpq,nqhc->nphc/dot_general | solution.py:91
  252.0 4.4 %fusion.62 = f32[8,128,4,64]{1,3,2,0:T(8,128)} fusion(bf16[8,128,4,64]{1,3,2,0:T(8,128)(2,1)S(1)} %bitcast.114, f32[8,128,4,64]{1,3,2,0:T(8,128)} %get-tuple-element.477, f32[8,128,128]{2,1,0:T(8,128)S(1)} %get-tuple-element.445, f32[4]{0:T(128)S(1)} %get-tuple-element.446, f32[8,128,128]{2,1,0:T(8,128)S(1)} %get-tuple-element.447, ...), kind=kOutput, calls=%fused_computation.2.clone.1 | convolution fusion | flops 76546048 | bytes 7340161 | tf_op jit(solution)/shard_map/while/body/eval_jaxpr/nhpq,nqhc->nphc/dot_general | solution.py:91
  262.8 4.4 %fusion.62 = f32[8,128,4,64]{1,3,2,0:T(8,128)} fusion(bf16[8,128,4,64]{1,3,2,0:T(8,128)(2,1)S(1)} %bitcast.114, f32[8,128,4,64]{1,3,2,0:T(8,128)} %get-tuple-element.477, f32[8,128,128]{2,1,0:T(8,128)S(1)} %get-tuple-element.445, f32[4]{0:T(128)S(1)} %get-tuple-element.446, f32[8,128,128]{2,1,0:T(8,128)S(1)} %get-tuple-element.447, ...), kind=kOutput, calls=%fused_computation.2.clone.1 | convolution fusion | flops 76546048 | bytes 7340161 | tf_op jit(solution)/shard_map/while/body/eval_jaxpr/nhpq,nqhc->nphc/dot_general | solution.py:91
  273.6 4.4 %fusion.62 = f32[8,128,4,64]{1,3,2,0:T(8,128)} fusion(bf16[8,128,4,64]{1,3,2,0:T(8,128)(2,1)S(1)} %bitcast.114, f32[8,128,4,64]{1,3,2,0:T(8,128)} %get-tuple-element.477, f32[8,128,128]{2,1,0:T(8,128)S(1)} %get-tuple-element.445, f32[4]{0:T(128)S(1)} %get-tuple-element.446, f32[8,128,128]{2,1,0:T(8,128)S(1)} %get-tuple-element.447, ...), kind=kOutput, calls=%fused_computation.2.clone.1 | convolution fusion | flops 76546048 | bytes 7340161 | tf_op jit(solution)/shard_map/while/body/eval_jaxpr/nhpq,nqhc->nphc/dot_general | solution.py:91
  284.3 4.4 %fusion.62 = f32[8,128,4,64]{1,3,2,0:T(8,128)} fusion(bf16[8,128,4,64]{1,3,2,0:T(8,128)(2,1)S(1)} %bitcast.114, f32[8,128,4,64]{1,3,2,0:T(8,128)} %get-tuple-element.477, f32[8,128,128]{2,1,0:T(8,128)S(1)} %get-tuple-element.445, f32[4]{0:T(128)S(1)} %get-tuple-element.446, f32[8,128,128]{2,1,0:T(8,128)S(1)} %get-tuple-element.447, ...), kind=kOutput, calls=%fused_computation.2.clone.1 | convolution fusion | flops 76546048 | bytes 7340161 | tf_op jit(solution)/shard_map/while/body/eval_jaxpr/nhpq,nqhc->nphc/dot_general | solution.py:91
  295.1 4.4 %fusion.62 = f32[8,128,4,64]{1,3,2,0:T(8,128)} fusion(bf16[8,128,4,64]{1,3,2,0:T(8,128)(2,1)S(1)} %bitcast.114, f32[8,128,4,64]{1,3,2,0:T(8,128)} %get-tuple-element.477, f32[8,128,128]{2,1,0:T(8,128)S(1)} %get-tuple-element.445, f32[4]{0:T(128)S(1)} %get-tuple-element.446, f32[8,128,128]{2,1,0:T(8,128)S(1)} %get-tuple-element.447, ...), kind=kOutput, calls=%fused_computation.2.clone.1 | convolution fusion | flops 76546048 | bytes 7340161 | tf_op jit(solution)/shard_map/while/body/eval_jaxpr/nhpq,nqhc->nphc/dot_general | solution.py:91
  305.9 4.4 %fusion.62 = f32[8,128,4,64]{1,3,2,0:T(8,128)} fusion(bf16[8,128,4,64]{1,3,2,0:T(8,128)(2,1)S(1)} %bitcast.114, f32[8,128,4,64]{1,3,2,0:T(8,128)} %get-tuple-element.477, f32[8,128,128]{2,1,0:T(8,128)S(1)} %get-tuple-element.445, f32[4]{0:T(128)S(1)} %get-tuple-element.446, f32[8,128,128]{2,1,0:T(8,128)S(1)} %get-tuple-element.447, ...), kind=kOutput, calls=%fused_computation.2.clone.1 | convolution fusion | flops 76546048 | bytes 7340161 | tf_op jit(solution)/shard_map/while/body/eval_jaxpr/nhpq,nqhc->nphc/dot_general | solution.py:91
  316.6 4.4 %fusion.62 = f32[8,128,4,64]{1,3,2,0:T(8,128)} fusion(bf16[8,128,4,64]{1,3,2,0:T(8,128)(2,1)S(1)} %bitcast.114, f32[8,128,4,64]{1,3,2,0:T(8,128)} %get-tuple-element.477, f32[8,128,128]{2,1,0:T(8,128)S(1)} %get-tuple-element.445, f32[4]{0:T(128)S(1)} %get-tuple-element.446, f32[8,128,128]{2,1,0:T(8,128)S(1)} %get-tuple-element.447, ...), kind=kOutput, calls=%fused_computation.2.clone.1 | convolution fusion | flops 76546048 | bytes 7340161 | tf_op jit(solution)/shard_map/while/body/eval_jaxpr/nhpq,nqhc->nphc/dot_general | solution.py:91
  327.4 4.4 %fusion.62 = f32[8,128,4,64]{1,3,2,0:T(8,128)} fusion(bf16[8,128,4,64]{1,3,2,0:T(8,128)(2,1)S(1)} %bitcast.114, f32[8,128,4,64]{1,3,2,0:T(8,128)} %get-tuple-element.477, f32[8,128,128]{2,1,0:T(8,128)S(1)} %get-tuple-element.445, f32[4]{0:T(128)S(1)} %get-tuple-element.446, f32[8,128,128]{2,1,0:T(8,128)S(1)} %get-tuple-element.447, ...), kind=kOutput, calls=%fused_computation.2.clone.1 | convolution fusion | flops 76546048 | bytes 7340161 | tf_op jit(solution)/shard_map/while/body/eval_jaxpr/nhpq,nqhc->nphc/dot_general | solution.py:91
  338.2 4.4 %fusion.62 = f32[8,128,4,64]{1,3,2,0:T(8,128)} fusion(bf16[8,128,4,64]{1,3,2,0:T(8,128)(2,1)S(1)} %bitcast.114, f32[8,128,4,64]{1,3,2,0:T(8,128)} %get-tuple-element.477, f32[8,128,128]{2,1,0:T(8,128)S(1)} %get-tuple-element.445, f32[4]{0:T(128)S(1)} %get-tuple-element.446, f32[8,128,128]{2,1,0:T(8,128)S(1)} %get-tuple-element.447, ...), kind=kOutput, calls=%fused_computation.2.clone.1 | convolution fusion | flops 76546048 | bytes 7340161 | tf_op jit(solution)/shard_map/while/body/eval_jaxpr/nhpq,nqhc->nphc/dot_general | solution.py:91
  348.9 4.4 %fusion.62 = f32[8,128,4,64]{1,3,2,0:T(8,128)} fusion(bf16[8,128,4,64]{1,3,2,0:T(8,128)(2,1)S(1)} %bitcast.114, f32[8,128,4,64]{1,3,2,0:T(8,128)} %get-tuple-element.477, f32[8,128,128]{2,1,0:T(8,128)S(1)} %get-tuple-element.445, f32[4]{0:T(128)S(1)} %get-tuple-element.446, f32[8,128,128]{2,1,0:T(8,128)S(1)} %get-tuple-element.447, ...), kind=kOutput, calls=%fused_computation.2.clone.1 | convolution fusion | flops 76546048 | bytes 7340161 | tf_op jit(solution)/shard_map/while/body/eval_jaxpr/nhpq,nqhc->nphc/dot_general | solution.py:91
  356.3 41.7 %all_gather.3 = bf16[2,512,256]{2,1,0:T(8,128)(2,1)S(1)} all-gather(bf16[2,16,256]{2,1,0:T(8,128)(2,1)S(1)} %fusion.27), channel_id=1, replica_groups=mesh['gx'=4,'gy'=4,'gz'=2] {'gx','gy','gz'}, dimensions={1}, use_global_device_ids=true | all-gather | bytes 540672 | tf_op jit(solution)/shard_map/all_gather | solution.py:153
  (343 shorter events, 217.4 us)
Async XLA Ops:
  6.5 348.6 %copy-start = (f32[256,256]{1,0:T(8,128)S(1)}, f32[256,256]{1,0:T(8,128)}, u32[]{:S(2)}) copy-start(f32[256,256]{1,0:T(8,128)} %param.17) | copy-start | bytes 786436
  6.5 11.9 %copy-start.16 = (f32[3]{0:T(128)S(1)}, f32[3]{0:T(128)}, u32[]{:S(2)}) copy-start(f32[3]{0:T(128)} %constant.273) | copy-start | bytes 40
  6.5 11.9 %copy-start.9 = (bf16[2,4,1,3,128]{4,1,3,2,0:T(4,128)(2,1)S(1)}, bf16[2,4,1,3,128]{4,1,3,2,0:T(4,128)(2,1)}, u32[]{:S(2)}) copy-start(bf16[2,4,1,3,128]{4,1,3,2,0:T(4,128)(2,1)} %param.13) | copy-start | bytes 18436
  6.5 11.9 %copy-start.13 = (s32[3,512]{1,0:T(4,128)S(1)}, s32[3,512]{1,0:T(4,128)}, u32[]{:S(2)}) copy-start(s32[3,512]{1,0:T(4,128)} %param.15) | copy-start | bytes 18436
  6.5 348.6 %reduce-scatter.2.cloned.1.call-start = ((), (), s32[]{:S(2)}) async-start(), calls=%async_computation.1 | async-start | bytes 1081344 | tf_op jit(solution)/shard_map/reduce_scatter | solution.py:143
  8.0 42.8 %collective-permute-start.6 = (bf16[1,4,1,4,128]{4,1,0,3,2:T(4,128)(2,1)S(1)}, bf16[1,4,1,4,128]{4,1,0,3,2:T(4,128)(2,1)S(1)}, u32[]{:S(2)}, u32[]{:S(2)}) collective-permute-start(bf16[1,4,1,4,128]{4,1,0,3,2:T(4,128)(2,1)S(1)} %get-tuple-element.367), channel_id=1, source_target_pairs={{0,8},{8,16},{16,24},{24,0},{1,9},{9,17},{17,25},{25,1},{2,10},{10... | collective-permute-start | bytes 12296 | tf_op jit(solution)/shard_map/ppermute | solution.py:21
  11.1 39.8 %collective-permute-start.7 = (bf16[1,4,1,4,128]{4,1,0,3,2:T(4,128)(2,1)S(1)}, bf16[1,4,1,4,128]{4,1,0,3,2:T(4,128)(2,1)S(1)}, u32[]{:S(2)}, u32[]{:S(2)}) collective-permute-start(bf16[1,4,1,4,128]{4,1,0,3,2:T(4,128)(2,1)S(1)} %get-tuple-element.368), channel_id=1, source_target_pairs={{8,0},{16,8},{24,16},{0,24},{9,1},{17,9},{25,17},{1,25},{10,2},{18... | collective-permute-start | bytes 12296 | tf_op jit(solution)/shard_map/ppermute | solution.py:22
  14.5 16.6 %copy-start.12 = (s32[2,4,1,128]{3,2,1,0:T(1,128)S(1)}, s32[2,4,1,128]{3,2,1,0:T(1,128)}, u32[]{:S(2)}) copy-start(s32[2,4,1,128]{3,2,1,0:T(1,128)} %param.14) | copy-start | bytes 12292
  14.5 16.6 %copy-start.1 = (bf16[2,4,1,128,256]{4,3,2,1,0:T(8,128)(2,1)S(1)}, bf16[2,4,1,128,256]{4,3,2,1,0:T(8,128)(2,1)}, u32[]{:S(2)}) copy-start(bf16[2,4,1,128,256]{4,3,2,1,0:T(8,128)(2,1)} %param.12) | copy-start | bytes 1572868
  14.5 13.2 %collective-permute-start = (bf16[1,4,1,128,256]{3,4,1,0,2:T(8,128)(2,1)S(1)}, bf16[1,4,1,128,256]{3,4,1,0,2:T(8,128)(2,1)S(1)}, u32[]{:S(2)}, u32[]{:S(2)}) collective-permute-start(bf16[1,4,1,128,256]{3,4,1,0,2:T(8,128)(2,1)S(1)} %get-tuple-element.358), channel_id=1, source_target_pairs={{0,8},{8,16},{16,24},{24,0},{1,9},{9,17},{17,25},{25,1},{2,10},{10... | collective-permute-start | bytes 786440 | tf_op jit(solution)/shard_map/ppermute | solution.py:21
  14.6 13.4 %collective-permute-start.1 = (bf16[1,4,1,128,256]{3,4,1,0,2:T(8,128)(2,1)S(1)}, bf16[1,4,1,128,256]{3,4,1,0,2:T(8,128)(2,1)S(1)}, u32[]{:S(2)}, u32[]{:S(2)}) collective-permute-start(bf16[1,4,1,128,256]{3,4,1,0,2:T(8,128)(2,1)S(1)} %get-tuple-element.359), channel_id=1, source_target_pairs={{8,0},{16,8},{24,16},{0,24},{9,1},{17,9},{25,17},{1,25},{10,2},{18... | collective-permute-start | bytes 786440 | tf_op jit(solution)/shard_map/ppermute | solution.py:22
  27.7 15.8 %copy-start.3 = (bf16[1024,512]{1,0:T(8,128)(2,1)}, bf16[1024,512]{1,0:T(8,128)(2,1)S(1)}, u32[]{:S(2)}) copy-start(bf16[1024,512]{1,0:T(8,128)(2,1)S(1)} %get-tuple-element.360) | copy-start | bytes 3145732
  27.7 15.8 %copy-start.5 = (bf16[1024,512]{1,0:T(8,128)(2,1)}, bf16[1024,512]{1,0:T(8,128)(2,1)S(1)}, u32[]{:S(2)}) copy-start(bf16[1024,512]{1,0:T(8,128)(2,1)S(1)} %get-tuple-element.361) | copy-start | bytes 3145732
  28.1 10.1 %collective-permute-start.2 = (bf16[4,1,1,128,256]{3,4,1,0,2:T(8,128)(2,1)S(1)}, bf16[4,1,1,128,256]{3,4,1,0,2:T(8,128)(2,1)S(1)}, u32[]{:S(2)}, u32[]{:S(2)}) collective-permute-start(bf16[4,1,1,128,256]{3,4,1,0,2:T(8,128)(2,1)S(1)} %get-tuple-element.356), channel_id=1, source_target_pairs={{0,2},{2,4},{4,6},{6,0},{1,3},{3,5},{5,7},{7,1},{8,10},{10,12},{12... | collective-permute-start | bytes 786440 | tf_op jit(solution)/shard_map/ppermute | solution.py:21
  29.7 12.0 %collective-permute-start.3 = (bf16[4,1,1,128,256]{3,4,1,0,2:T(8,128)(2,1)S(1)}, bf16[4,1,1,128,256]{3,4,1,0,2:T(8,128)(2,1)S(1)}, u32[]{:S(2)}, u32[]{:S(2)}) collective-permute-start(bf16[4,1,1,128,256]{3,4,1,0,2:T(8,128)(2,1)S(1)} %get-tuple-element.357), channel_id=1, source_target_pairs={{2,0},{4,2},{6,4},{0,6},{3,1},{5,3},{7,5},{1,7},{10,8},{12,10},{14... | collective-permute-start | bytes 786440 | tf_op jit(solution)/shard_map/ppermute | solution.py:22
  38.2 5.3 %copy-start.7 = (bf16[4,1,1,128,256]{3,4,1,0,2:T(8,128)(2,1)}, bf16[4,1,1,128,256]{3,4,1,0,2:T(8,128)(2,1)S(1)}, u32[]{:S(2)}) copy-start(bf16[4,1,1,128,256]{3,4,1,0,2:T(8,128)(2,1)S(1)} %collective-permute-done.2) | copy-start | bytes 786436
  41.6 1.9 copy-start.8
  43.0 14.6 %collective-permute-start.4 = (bf16[4,6,1,128,256]{3,4,1,0,2:T(8,128)(2,1)}, bf16[4,6,1,128,256]{3,4,1,0,2:T(8,128)(2,1)}, u32[]{:S(2)}, u32[]{:S(2)}) collective-permute-start(bf16[4,6,1,128,256]{3,4,1,0,2:T(8,128)(2,1)} %pad_maximum_fusion.2), channel_id=1, source_target_pairs={{0,1},{1,0},{2,3},{3,2},{4,5},{5,4},{6,7},{7,6},{8,9},{9,8},{10,11... | collective-permute-start | bytes 4718600 | tf_op jit(solution)/shard_map/ppermute | solution.py:21
  43.0 14.6 %collective-permute-start.5 = (bf16[4,6,1,128,256]{3,4,1,0,2:T(8,128)(2,1)}, bf16[4,6,1,128,256]{3,4,1,0,2:T(8,128)(2,1)}, u32[]{:S(2)}, u32[]{:S(2)}) collective-permute-start(bf16[4,6,1,128,256]{3,4,1,0,2:T(8,128)(2,1)} %pad_maximum_fusion.2), channel_id=1, source_target_pairs={{1,0},{0,1},{3,2},{2,3},{5,4},{4,5},{7,6},{6,7},{9,8},{8,9},{11,10... | collective-permute-start | bytes 4718600 | tf_op jit(solution)/shard_map/ppermute | solution.py:22
  48.0 8.7 %copy-start.14 = (f32[8,4]{0,1:T(4,128)S(1)}, f32[8,4]{0,1:T(4,128)}, u32[]{:S(2)}) copy-start(f32[8,4]{0,1:T(4,128)} %param.16) | copy-start | bytes 388
  50.9 4.6 %collective-permute-start.8 = (bf16[4,1,1,4,128]{4,1,0,3,2:T(2,128)(2,1)S(1)}, bf16[4,1,1,4,128]{4,1,0,3,2:T(2,128)(2,1)S(1)}, u32[]{:S(2)}, u32[]{:S(2)}) collective-permute-start(bf16[4,1,1,4,128]{4,1,0,3,2:T(2,128)(2,1)S(1)} %get-tuple-element.362), channel_id=1, source_target_pairs={{0,2},{2,4},{4,6},{6,0},{1,3},{3,5},{5,7},{7,1},{8,10},{10,12},{12... | collective-permute-start | bytes 12296 | tf_op jit(solution)/shard_map/ppermute | solution.py:21
  52.4 3.7 collective-permute-start.9
  56.1 1.3 collective-permute-start.10
  56.2 1.4 collective-permute-start.11
  353.3 1.8 copy-start.15
  353.3 44.7 %copy-start.10 = (bf16[256,256]{1,0:T(8,128)(2,1)S(1)}, bf16[256,256]{1,0:T(8,128)(2,1)}, u32[]{:S(2)}) copy-start(bf16[256,256]{1,0:T(8,128)(2,1)} %param.18) | copy-start | bytes 393220
  354.7 44.6 %copy-start.4 = (bf16[1024,512]{1,0:T(8,128)(2,1)S(1)}, bf16[1024,512]{1,0:T(8,128)(2,1)}, u32[]{:S(2)}) copy-start(bf16[1024,512]{1,0:T(8,128)(2,1)} %copy-done.3) | copy-start | bytes 3145732
  354.7 44.6 %copy-start.6 = (bf16[1024,512]{1,0:T(8,128)(2,1)S(1)}, bf16[1024,512]{1,0:T(8,128)(2,1)}, u32[]{:S(2)}) copy-start(bf16[1024,512]{1,0:T(8,128)(2,1)} %copy-done.5) | copy-start | bytes 3145732
  399.4 3.2 copy-start.2
  399.4 3.2 copy-start.11
Sparse Core Ops, SparseCore 0:
  50.9 135.6 reduce-scatter.1
where the time goes:
time: 414 us; the launch traced here: 412 us
  other arithmetic  133 us (32%)
  matrix products  128 us (31%)
  local copies, waits for them, and re-layouts  66.1 us (16%)
  blocking collectives  41.7 us (10%)
  starting transfers between devices  16.1 us (4%)
  between operations  13.7 us (3%)
  waiting for transfers between devices  12.2 us (3%)
    dot_general x27, matrix products, add_offset(): jnp.einsum('nhpq,nqhc->nphc', weights, near_feat, preferred_element_type=...  117 us
    exp x27, other arithmetic, pair_weights(): jnp.exp(-sharpness * jnp.square(distance - level_id / (level_count - 1)))  59.6 us
    sub x27, other arithmetic, pair_weights(): near_geom[:, axis_id, None, :] + shift_vec[axis_id]  49.2 us
    all_gather x1, blocking collectives, body(): lax.all_gather((mixed_rows * share_damp[None, :, None]).astype(jnp.bfloat...  41.7 us
    dynamic_slice x27, local copies, waits for them, and re-layouts, add_offset(): lax.dynamic_slice(wide_feat, (step_x + 1, step_y + 1, step_z + 1, anchor,...  29.1 us
    slice x27, local copies, waits for them, and re-layouts, pair_weights(): shift_vec[axis_id]  16.6 us
    mul x27, local copies, waits for them, and re-layouts, pair_weights(): radial_bump[:, None] * radial_weight[level_id][None, :, None, None]  14.7 us
    ppermute x6, starting transfers between devices, padded(): after = lax.ppermute(first, axis, down)  9.77 us
  transfers between devices with their start and end apart: 13, of which 6 were waited for; matrix products, arithmetic and copies ran while one was open for 77% of the time, Pallas kernels for 0%

commit v1 on v0

v1 whole, which is shorter than its diff:
```python
import functools
import math

import jax
import jax.numpy as jnp
from jax import lax
from jax.experimental import pallas as pl
from jax.experimental.pallas import tpu as pltpu
from jax.sharding import PartitionSpec as P

sharpness = 16.0
smearing = 0.04
screening = 4.0
strength = 24.0

SIN_C = [(-1.0) ** k * math.pi ** (2 * k + 1) / math.factorial(2 * k + 1) for k in range(7)]
COS_C = [(-1.0) ** k * math.pi ** (2 * k) / math.factorial(2 * k) for k in range(7)]


def poly(z, coefs):
    acc = jnp.full_like(z, coefs[-1])
    for c in coefs[-2::-1]:
        acc = acc * z + c
    return acc


def shifted(x, axis, dim, width):
    count, length = lax.axis_size(axis), x.shape[dim]
    up = [(i, (i + 1) % count) for i in range(count)]
    down = [(j, i) for i, j in up]
    last = lax.slice_in_dim(x, length - width, length, axis=dim)
    first = lax.slice_in_dim(x, 0, width, axis=dim)
    return lax.ppermute(last, axis, up), lax.ppermute(first, axis, down)


def widen(x, axis, dim):
    before, after = shifted(x, axis, dim, 1)
    return jnp.concatenate([before, x, after], axis=dim)


def message_kernel(cells_y, cells_z, fold_z, levels, home_ref, feat_ref, geom_ref, wb_ref, out_ref, hb, phi, acc):
    cell = pl.program_id(0)
    x = cell // (cells_y * cells_z)
    y = (cell // cells_z) % cells_y
    z = cell % cells_z
    slots = out_ref.shape[1]
    feat = out_ref.shape[2]
    near_z = feat_ref.shape[3]
    chunk = 32
    for a in range(3):
        hb[a] = jnp.broadcast_to(home_ref[0, :, a : a + 1], (slots, slots))
    for ox in range(3):
        for oy in range(3):
            for oz in range(near_z):
                g = geom_ref[x + ox, z, y + oy, oz]
                nx = g[0:1] + (ox - 1.0)
                ny = g[1:2] + (oy - 1.0)
                if fold_z:
                    nz = g[2:3]
                else:
                    nz = g[2:3] + (oz - 1.0)
                col = (oy * near_z + oz) * slots
                center = ox == 1 and oy == 1 and oz == (0 if fold_z else 1)
                for p0 in range(0, slots, chunk):
                    dx = nx - hb[0, p0 : p0 + chunk]
                    dy = ny - hb[1, p0 : p0 + chunk]
                    dz = nz - hb[2, p0 : p0 + chunk]
                    if fold_z and oz == 1:
                        dz = 1.0 - jnp.abs(dz)
                    sq = jnp.minimum(dx * dx + dy * dy + dz * dz, 1.0)
                    dist = sq * lax.rsqrt(jnp.maximum(sq, 1e-30))
                    ratio = jnp.exp2(dist * (2.0 * sharpness / (levels - 1) * math.log2(math.e)))
                    edge = 1.0 - sq
                    val = edge * edge * jnp.exp2(sq * (-sharpness * math.log2(math.e)))
                    if center:
                        row = lax.broadcasted_iota(jnp.int32, val.shape, 0) + p0
                        lane = lax.broadcasted_iota(jnp.int32, val.shape, 1)
                        val = jnp.where(row == lane, 0.0, val)
                    for b in range(levels):
                        phi[ox, b * slots + p0 : b * slots + p0 + chunk, col : col + slots] = val.astype(jnp.bfloat16)
                        if b + 1 < levels:
                            val = val * ratio
        rows = feat_ref[x + ox, z, pl.ds(y, 3)].reshape(3 * near_z * slots, feat)
        part = jnp.dot(phi[ox], rows, preferred_element_type=jnp.float32)
        if ox == 0:
            acc[...] = part
        elif ox == 1:
            acc[...] += part
    total = jnp.zeros((slots, feat), jnp.float32)
    for b in range(levels):
        both = acc[b * slots : (b + 1) * slots] + part[b * slots : (b + 1) * slots]
        total = total + both * wb_ref[b : b + 1]
    out_ref[0] = total.astype(jnp.bfloat16)


def basis_kernel(pos_ref, wave_ref, feat_ref, basis_ref, struct_ref):
    cell = pl.program_id(0)
    waves = wave_ref.shape[0]
    pos = pos_ref[0]
    chunk = 64
    for w0 in range(0, waves, chunk):
        wv = wave_ref[w0 : w0 + chunk]
        turns = wv[:, 0:1] * pos[0:1] + wv[:, 1:2] * pos[1:2] + wv[:, 2:3] * pos[2:3]
        u = turns - jnp.floor(turns + 0.5)
        q = u * u
        s = u * poly(q, SIN_C)
        c = poly(q, COS_C)
        basis_ref[0, w0 : w0 + chunk] = (1.0 - 2.0 * s * s).astype(jnp.bfloat16)
        basis_ref[0, waves + w0 : waves + w0 + chunk] = (2.0 * s * c).astype(jnp.bfloat16)
    part = jnp.dot(basis_ref[0], feat_ref[0], preferred_element_type=jnp.float32)

    @pl.when(cell == 0)
    def _():
        struct_ref[...] = part

    @pl.when(cell > 0)
    def _():
        struct_ref[...] += part


def final_kernel(basis_ref, grid_ref, msg_ref, feat_ref, home_ref, wm_ref, wo_ref, out_ref):
    far = lax.dot_general(
        basis_ref[0], grid_ref[...], (((0,), (0,)), ((), ())), preferred_element_type=jnp.float32
    )
    joined = far + jnp.dot(msg_ref[0], wm_ref[...], preferred_element_type=jnp.float32)
    hidden = (joined / (1.0 + jnp.exp(-joined))).astype(jnp.bfloat16)
    result = feat_ref[0].astype(jnp.float32) + jnp.dot(hidden, wo_ref[...], preferred_element_type=jnp.float32)
    out_ref[0] = (result * home_ref[0, :, 3:4]).astype(jnp.bfloat16)


def body(
    features,
    fractions,
    occupied,
    wave_index,
    radial_weight,
    ewald_mix,
    msg_weight,
    ewald_weight,
    out_weight,
):
    cx, cy, cz, slots, feat = features.shape
    levels, heads = radial_weight.shape
    cells = cx * cy * cz
    grid = [lax.axis_size("gx") * cx, lax.axis_size("gy") * cy, lax.axis_size("gz") * cz]
    devices = lax.axis_size("gx") * lax.axis_size("gy") * lax.axis_size("gz")
    waves = wave_index.shape[1]
    axes = ("gx", "gy", "gz")
    full = lambda shape: pl.BlockSpec(shape, lambda i: (0,) * len(shape))
    params = pltpu.CompilerParams(dimension_semantics=("arbitrary",), vmem_limit_bytes=56 * 2**20)

    masked = features * occupied[..., None].astype(jnp.bfloat16)
    frac = fractions.astype(jnp.float32)
    cell_feat = masked.reshape(cells, slots, feat)
    home = jnp.concatenate([frac, occupied[:, :, :, None, :].astype(jnp.float32)], axis=3)
    home = jnp.swapaxes(home.reshape(cells, 4, slots), 1, 2)

    start = [
        (lax.axis_index(n) * c + jnp.arange(c, dtype=jnp.int32)).astype(jnp.float32)
        for n, c in zip(axes, (cx, cy, cz))
    ]
    origin = jnp.stack(jnp.meshgrid(*start, indexing="ij"), axis=-1)[..., None]
    pos = (origin + frac).reshape(cells, 3, slots)
    lengths = jnp.array(grid, jnp.float32)
    index = wave_index.astype(jnp.float32)
    wave_vec = 2.0 * math.pi * index / lengths[:, None]
    wave_sq = jnp.sum(wave_vec * wave_vec, axis=0)
    damping = (
        strength
        * jnp.exp(-0.5 * smearing * wave_sq)
        / (wave_sq + screening)
        * (1.0 / math.sqrt(cells * slots * devices * waves))
    )
    wave_turn = (index / lengths[:, None]).T

    basis, struct = pl.pallas_call(
        basis_kernel,
        grid=(cells,),
        in_specs=[
            pl.BlockSpec((1, 3, slots), lambda i: (i, 0, 0)),
            full((waves, 3)),
            pl.BlockSpec((1, slots, feat), lambda i: (i, 0, 0)),
        ],
        out_specs=[pl.BlockSpec((1, 2 * waves, slots), lambda i: (i, 0, 0)), full((2 * waves, feat))],
        out_shape=[
            jax.ShapeDtypeStruct((cells, 2 * waves, slots), jnp.bfloat16),
            jax.ShapeDtypeStruct((2 * waves, feat), jnp.float32),
        ],
        compiler_params=params,
        name="basis",
    )(pos, wave_turn, cell_feat)

    wave_share = lax.psum_scatter(struct.reshape(2, waves, feat), axes, scatter_dimension=1, tiled=True)
    share_rows = wave_share.shape[1]
    share_damp = lax.dynamic_slice_in_dim(damping, lax.axis_index(axes) * share_rows, share_rows, 0)
    mixed = jnp.dot(wave_share.reshape(2 * share_rows, feat), ewald_mix, precision=lax.Precision.HIGHEST)
    filtered = (mixed.reshape(2, share_rows, feat) * share_damp[None, :, None]).astype(jnp.bfloat16)
    projected = jnp.dot(filtered, ewald_weight, preferred_element_type=jnp.float32).astype(jnp.bfloat16)
    field = lax.all_gather(projected, axes, axis=1, tiled=True).reshape(2 * waves, feat)

    fold_z = grid[2] == 2 and cz == 1
    wide_feat = widen(widen(masked, "gx", 0), "gy", 1)
    wide_geom = widen(widen(fractions, "gx", 0), "gy", 1)
    if fold_z:
        swap = [(0, 1), (1, 0)]
        wide_feat = jnp.concatenate([wide_feat, lax.ppermute(wide_feat, "gz", swap)], axis=2)
        wide_geom = jnp.concatenate([wide_geom, lax.ppermute(wide_geom, "gz", swap)], axis=2)
        near_z = 2
    else:
        wide_feat = widen(wide_feat, "gz", 2)
        wide_geom = widen(wide_geom, "gz", 2)
        near_z = 3
    wide_feat = jnp.stack([wide_feat[:, :, z : z + near_z] for z in range(cz)], axis=1)
    wide_geom = jnp.stack([wide_geom[:, :, z : z + near_z] for z in range(cz)], axis=1).astype(jnp.float32)
    level = jnp.arange(levels, dtype=jnp.float32) / (levels - 1)
    wb = radial_weight * (jnp.exp(-sharpness * level * level) / math.sqrt(4.0 * slots))[:, None]
    wb = jnp.repeat(wb, feat // heads, axis=1)
    messages = pl.pallas_call(
        functools.partial(message_kernel, cy, cz, fold_z, levels),
        grid=(cells,),
        in_specs=[
            pl.BlockSpec((1, slots, 4), lambda i: (i, 0, 0)),
            full(wide_feat.shape),
            full(wide_geom.shape),
            full(wb.shape),
        ],
        out_specs=pl.BlockSpec((1, slots, feat), lambda i: (i, 0, 0)),
        out_shape=jax.ShapeDtypeStruct((cells, slots, feat), jnp.bfloat16),
        scratch_shapes=[
            pltpu.VMEM((3, slots, slots), jnp.float32),
            pltpu.VMEM((3, levels * slots, 3 * near_z * slots), jnp.bfloat16),
            pltpu.VMEM((levels * slots, feat), jnp.float32),
        ],
        compiler_params=params,
        cost_estimate=pl.CostEstimate(
            flops=2 * cells * levels * slots * 9 * near_z * slots * feat, bytes_accessed=2**22, transcendentals=0
        ),
        name="messages",
    )(home, wide_feat, wide_geom, wb)

    out = pl.pallas_call(
        final_kernel,
        grid=(cells,),
        in_specs=[
            pl.BlockSpec((1, 2 * waves, slots), lambda i: (i, 0, 0)),
            full((2 * waves, feat)),
            pl.BlockSpec((1, slots, feat), lambda i: (i, 0, 0)),
            pl.BlockSpec((1, slots, feat), lambda i: (i, 0, 0)),
            pl.BlockSpec((1, slots, 4), lambda i: (i, 0, 0)),
            full((feat, feat)),
            full((feat, feat)),
        ],
        out_specs=pl.BlockSpec((1, slots, feat), lambda i: (i, 0, 0)),
        out_shape=jax.ShapeDtypeStruct((cells, slots, feat), jnp.bfloat16),
        compiler_params=params,
        name="final",
    )(basis, field, messages, cell_feat, home, msg_weight, out_weight)
    return out.reshape(features.shape)


def solution(mesh):
    cell = P("gx", "gy", "gz", None, None)
    in_specs = (cell, cell, P("gx", "gy", "gz", None), P(), P(), P(), P(), P(), P())
    return jax.shard_map(body, mesh=mesh, in_specs=in_specs, out_specs=cell, check_vma=False)
```

time: 414 us -> 241 us (0.58)
  matrix products: 128 us -> 1.13 us
  other arithmetic: 133 us -> 11 us
  waiting for transfers between devices: 12.2 us -> 114 us
  local copies, waits for them, and re-layouts: 66.1 us -> 9.46 us
  Pallas kernels: 0 us -> 35.2 us
    dot_general x32 -> x2, matrix products: 128 us -> 1.13 us  [the longest x1 0.99 us: body(): jnp.dot(wave_share.reshape(2 * share_rows, feat), ewald_mix, precision=la...]
    reduce_scatter x1, waiting for transfers between devices: 0.02 us -> 102 us  [body(): lax.psum_scatter(struct.reshape(2, waves, feat), axes, scatter_dimension=...]
    exp x27 -> x0, other arithmetic: 59.6 us -> none  [pair_weights(): jnp.exp(-sharpness * jnp.square(distance - level_id / (level_count - 1)))]
    sub x54 -> x0, other arithmetic: 49.6 us -> none  [the longest x27 49.2 us: pair_weights(): near_geom[:, axis_id, None, :] + shift_vec[axis_id]]
    pallas_call x0 -> x3, Pallas kernels: none -> 35.2 us  [the longest x1 19.3 us: body(): pl.pallas_call(functools.partial(message_kernel, cy, cz, fold_z, levels),...]
    dynamic_slice x55 -> x1, local copies, waits for them, and re-layouts: 30 us -> 1.32 us  [body(): lax.dynamic_slice_in_dim(damping, lax.axis_index(axes) * share_rows, shar...]
    slice x31 -> x3, local copies, waits for them, and re-layouts: 16.6 us -> 0.64 us  [the longest x2 0.63 us: shifted(): last = lax.slice_in_dim(x, length - width, length, axis=dim)]
    mul x27 -> x1, local copies, waits for them, and re-layouts: 14.7 us -> 1.33 us  [body(): radial_weight * (jnp.exp(-sharpness * level * level) / math.sqrt(4.0 * sl...]
  transfers between devices with their start and end apart: 13 -> 11, of which waited for: 6 -> 4; matrix products, arithmetic and copies ran while one was open for 77% -> 7% of each run, Pallas kernels for 0% -> 4%
where the time goes in v1:
time: 241 us; the launch traced here: 240 us
  waiting for transfers between devices  114 us (47%)
  blocking collectives  40.4 us (17%)
  Pallas kernels  35.2 us (15%)
  starting transfers between devices  15.1 us (6%)
  between operations  13.6 us (6%)
  other arithmetic  11 us (5%)
  local copies, waits for them, and re-layouts  9.46 us (4%)
    reduce_scatter x1, waiting for transfers between devices, body(): lax.psum_scatter(struct.reshape(2, waves, feat), axes, scatter_dimension=...  102 us
    all_gather x1, blocking collectives, body(): lax.all_gather(projected, axes, axis=1, tiled=True).reshape(2 * waves, feat)  40.4 us
    pallas_call x1, Pallas kernels, body(): pl.pallas_call(functools.partial(message_kernel, cy, cz, fold_z, levels),...  19.3 us
    ppermute x8, starting transfers between devices, shifted(): return (lax.ppermute(last, axis, up), lax.ppermute(first, axis, down))  15 us
    ppermute x8, waiting for transfers between devices, shifted(): return (lax.ppermute(last, axis, up), lax.ppermute(first, axis, down))  11.8 us
    pallas_call x1, Pallas kernels, body(): pl.pallas_call(basis_kernel, grid=(cells,), in_specs=[pl.BlockSpec((1, 3,...  8.5 us
    pallas_call x1, Pallas kernels, body(): pl.pallas_call(final_kernel, grid=(cells,), in_specs=[pl.BlockSpec((1, 2...  7.43 us
  transfers between devices with their start and end apart: 11, of which 4 were waited for; matrix products, arithmetic and copies ran while one was open for 7% of the time, Pallas kernels for 4%

profile of v1, /device:TPU:0, one launch (start us, length us, event | category | flops | bytes accessed | tf_op | source)
XLA Modules:
  0.0 239.8 jit_solution(2577143551570383982)
XLA Ops:
  6.6 1.4 fusion.11
  8.0 1.3 broadcast_multiply_fusion
  9.3 3.1 %collective-permute-start = (bf16[1,4,1,128,256]{4,3,2,1,0:T(8,128)(2,1)S(1)}, bf16[1,4,1,128,256]{4,3,2,1,0:T(8,128)(2,1)S(1)}, u32[]{:S(2)}, u32[]{:S(2)}) collective-permute-start(bf16[1,4,1,128,256]{4,3,2,1,0:T(8,128)(2,1)S(1)} %get-tuple-element.11), channel_id=1, source_target_pairs={{0,8},{8,16},{16,24},{24,0},{1,9},{9,17},{17,25},{25,1},{2,10},{10... | collective-permute-start | bytes 786440 | tf_op jit(solution)/shard_map/ppermute | solution.py:33
  12.4 2.1 collective-permute-start.1
  14.8 0.6 copy.56
  15.5 0.9 copy.57
  16.3 8.5 %basis.1 = (bf16[8,1024,128]{2,1,0:T(8,128)(2,1)}, f32[1024,256]{1,0:T(8,128)}) custom-call(f32[8,3,128]{2,1,0:T(4,128)} %bitcast.39, f32[512,3]{1,0:T(8,128)} %bitcast.37, bf16[8,128,256]{2,1,0:T(8,128)(2,1)} %bitcast.32), custom_call_target="tpu_custom_call" | custom-call | tf_op jit(solution)/shard_map/basis/pallas_call | solution.py:176
  25.0 3.8 %collective-permute-start.6 = (bf16[1,4,1,3,128]{4,3,1,0,2:T(4,128)(2,1)S(1)}, bf16[1,4,1,3,128]{4,3,1,0,2:T(4,128)(2,1)S(1)}, u32[]{:S(2)}, u32[]{:S(2)}) collective-permute-start(bf16[1,4,1,3,128]{4,3,1,0,2:T(4,128)(2,1)S(1)} %copy.72), channel_id=1, source_target_pairs={{8,0},{16,8},{24,16},{0,24},{9,1},{17,9},{25,17},{1,25},{10,2},{18... | collective-permute-start | bytes 9224 | tf_op jit(solution)/shard_map/ppermute | solution.py:33
  29.4 1.0 pad_maximum_fusion.3
  30.4 1.7 collective-permute-start.2
  32.1 1.3 collective-permute-start.3
  33.4 0.6 fusion.4
  34.0 7.2 %collective-permute-done.2 = bf16[4,1,1,128,256]{4,3,2,1,0:T(8,128)(2,1)S(1)} collective-permute-done((bf16[4,1,1,128,256]{4,3,2,1,0:T(8,128)(2,1)S(1)}, bf16[4,1,1,128,256]{4,3,2,1,0:T(8,128)(2,1)S(1)}, u32[]{:S(2)}, u32[]{:S(2)}) %collective-permute-start.2) | collective-permute-done | bytes 262176 | tf_op jit(solution)/shard_map/ppermute | solution.py:33
  41.2 4.5 %collective-permute-done.3 = bf16[4,1,1,128,256]{4,3,2,1,0:T(8,128)(2,1)S(1)} collective-permute-done((bf16[4,1,1,128,256]{4,3,2,1,0:T(8,128)(2,1)S(1)}, bf16[4,1,1,128,256]{4,3,2,1,0:T(8,128)(2,1)S(1)}, u32[]{:S(2)}, u32[]{:S(2)}) %collective-permute-start.3) | collective-permute-done | bytes 262176 | tf_op jit(solution)/shard_map/ppermute | solution.py:33
  46.2 0.6 fusion.9
  46.8 1.5 collective-permute-start.7
  48.2 1.5 collective-permute-start.8
  49.7 0.6 pad_maximum_fusion.5
  50.3 1.7 copy.60
  52.0 1.3 copy.65
  53.4 1.4 broadcast_in_dim.2
  54.7 1.4 reshape.100.wb_ref
  56.1 1.3 dynamic_slice.3
  57.4 0.7 pad_maximum_fusion.4
  58.2 0.7 fusion.14
  59.4 0.7 maximum_convert_fusion.geom_ref
  60.1 101.6 %reduce-scatter.2.cloned.1.call-done = f32[2,16,256]{2,1,0:T(8,128)} async-done(((f32[2,512,256]{2,1,0:T(8,128)}), f32[2,16,256]{2,1,0:T(8,128)}) %reduce-scatter.2.cloned.1.call-update) | async-done | bytes 32784 | tf_op jit(solution)/shard_map/reduce_scatter | solution.py:193
  161.7 1.0 fusion
  162.8 40.4 %all_gather.3 = bf16[2,512,256]{2,1,0:T(8,128)(2,1)} all-gather(bf16[2,16,256]{2,1,0:T(8,128)(2,1)S(1)} %convolution_convert_fusion), channel_id=1, replica_groups=mesh['gx'=4,'gy'=4,'gz'=2] {'gx','gy','gz'}, dimensions={1}, use_global_device_ids=true | all-gather | bytes 540672 | tf_op jit(solution)/shard_map/all_gather | solution.py:199
  203.2 3.0 %maximum_bitcast_fusion.feat_ref = bf16[4,1,6,2,128,256]{5,4,3,2,1,0:T(8,128)(2,1)} fusion(bf16[4,6,1,128,256]{4,3,2,1,0:T(8,128)(2,1)} %collective-permute-done.4, bf16[4,1,1,128,256]{4,3,2,1,0:T(8,128)(2,1)S(1)} %collective-permute-done.3, bf16[1,4,1,128,256]{4,3,2,1,0:T(8,128)(2,1)S(1)} %collective-permute-done.1, ...), kind=kLoop, calls=%fused_computation | loop fusion | flops 7864320 | bytes 6291456 | tf_op jit(solution)/shard_map/stack | solution.py:213
  206.2 19.3 %messages.1.msg_ref = bf16[8,128,256]{2,1,0:T(8,128)(2,1)} custom-call(f32[8,128,4]{2,1,0:T(8,128)} %bitcast.34, bf16[4,1,6,2,128,256]{5,4,3,2,1,0:T(8,128)(2,1)} %maximum_bitcast_fusion.feat_ref, f32[4,1,6,2,3,128]{5,4,3,2,1,0:T(4,128)} %maximum_convert_fusion.geom_ref, f32[8,256]{1,0:T(8,128)} %reshape.100.wb_ref), custom_call_target="tpu_custom_call" | custom-call | flops 9663676416 | bytes 4194304 | tf_op jit(solution)/shard_map/messages/pallas_call | solution.py:218
  225.6 7.4 %final.1 = bf16[8,128,256]{2,1,0:T(8,128)(2,1)} custom-call(bf16[8,1024,128]{2,1,0:T(8,128)(2,1)} %get-tuple-element.7.basis_ref, bf16[1024,256]{1,0:T(8,128)(2,1)} %bitcast.36, bf16[8,128,256]{2,1,0:T(8,128)(2,1)} %messages.1.msg_ref, bf16[8,128,256]{2,1,0:T(8,128)(2,1)} %bitcast.33, f32[8,128,4]{2,1,0:T(8,128)} %bitcast.35, bf16[256,256]{1,0:T(8,128)(2,1)} %wm_ref.1, ...), custom_call_target="tpu_custom_call" | custom-call | tf_op jit(solution)/shard_map/final/pallas_call | solution.py:241
  (55 shorter events, 2.2 us)
Async XLA Ops:
  6.5 155.1 %copy-start = (f32[256,256]{1,0:T(8,128)S(1)}, f32[256,256]{1,0:T(8,128)}, u32[]{:S(2)}) copy-start(f32[256,256]{1,0:T(8,128)} %param.15) | copy-start | bytes 786436
  6.5 8.8 %copy-start.9 = (f32[3]{0:T(128)S(1)}, f32[3]{0:T(128)}, u32[]{:S(2)}) copy-start(f32[3]{0:T(128)} %constant.50) | copy-start | bytes 40
  6.5 8.2 %copy-start.4 = (bf16[2,4,1,3,128]{4,1,3,2,0:T(4,128)(2,1)S(1)}, bf16[2,4,1,3,128]{4,1,3,2,0:T(4,128)(2,1)}, u32[]{:S(2)}) copy-start(bf16[2,4,1,3,128]{4,1,3,2,0:T(4,128)(2,1)} %param.11) | copy-start | bytes 18436
  6.5 8.8 %copy-start.7 = (s32[3,512]{1,0:T(4,128)S(1)}, s32[3,512]{1,0:T(4,128)}, u32[]{:S(2)}) copy-start(s32[3,512]{1,0:T(4,128)} %param.13) | copy-start | bytes 18436
  6.5 155.1 %reduce-scatter.2.cloned.1.call-start = ((), (), s32[]{:S(2)}) async-start(), calls=%async_computation.1 | async-start | bytes 1081344 | tf_op jit(solution)/shard_map/reduce_scatter | solution.py:193
  7.9 20.8 %copy-start.8 = (f32[8,4]{0,1:T(4,128)S(1)}, f32[8,4]{0,1:T(4,128)}, u32[]{:S(2)}) copy-start(f32[8,4]{0,1:T(4,128)} %param.14) | copy-start | bytes 388
  9.2 7.1 %copy-start.1 = (bf16[2,4,1,128,256]{4,3,2,1,0:T(8,128)(2,1)}, bf16[2,4,1,128,256]{4,3,2,1,0:T(8,128)(2,1)S(1)}, u32[]{:S(2)}) copy-start(bf16[2,4,1,128,256]{4,3,2,1,0:T(8,128)(2,1)S(1)} %broadcast_multiply_fusion) | copy-start | bytes 1572868
  9.3 20.1 %collective-permute-start = (bf16[1,4,1,128,256]{4,3,2,1,0:T(8,128)(2,1)S(1)}, bf16[1,4,1,128,256]{4,3,2,1,0:T(8,128)(2,1)S(1)}, u32[]{:S(2)}, u32[]{:S(2)}) collective-permute-start(bf16[1,4,1,128,256]{4,3,2,1,0:T(8,128)(2,1)S(1)} %get-tuple-element.11), channel_id=1, source_target_pairs={{0,8},{8,16},{16,24},{24,0},{1,9},{9,17},{17,25},{25,1},{2,10},{10... | collective-permute-start | bytes 786440 | tf_op jit(solution)/shard_map/ppermute | solution.py:33
  12.4 17.0 %collective-permute-start.1 = (bf16[1,4,1,128,256]{4,3,2,1,0:T(8,128)(2,1)S(1)}, bf16[1,4,1,128,256]{4,3,2,1,0:T(8,128)(2,1)S(1)}, u32[]{:S(2)}, u32[]{:S(2)}) collective-permute-start(bf16[1,4,1,128,256]{4,3,2,1,0:T(8,128)(2,1)S(1)} %get-tuple-element.12), channel_id=1, source_target_pairs={{8,0},{16,8},{24,16},{0,24},{9,1},{17,9},{25,17},{1,25},{10,2},{18... | collective-permute-start | bytes 786440 | tf_op jit(solution)/shard_map/ppermute | solution.py:33
  24.8 21.0 %copy-start.2 = (bf16[2,4,1,128,256]{4,3,2,1,0:T(8,128)(2,1)S(1)}, bf16[2,4,1,128,256]{4,3,2,1,0:T(8,128)(2,1)}, u32[]{:S(2)}) copy-start(bf16[2,4,1,128,256]{4,3,2,1,0:T(8,128)(2,1)} %copy-done.1) | copy-start | bytes 1572868
  24.9 9.1 %collective-permute-start.5 = (bf16[1,4,1,3,128]{4,3,1,0,2:T(4,128)(2,1)S(1)}, bf16[1,4,1,3,128]{4,3,1,0,2:T(4,128)(2,1)S(1)}, u32[]{:S(2)}, u32[]{:S(2)}) collective-permute-start(bf16[1,4,1,3,128]{4,3,1,0,2:T(4,128)(2,1)S(1)} %copy.71), channel_id=1, source_target_pairs={{0,8},{8,16},{16,24},{24,0},{1,9},{9,17},{17,25},{25,1},{2,10},{10... | collective-permute-start | bytes 9224 | tf_op jit(solution)/shard_map/ppermute | solution.py:33
  25.0 21.2 %collective-permute-start.6 = (bf16[1,4,1,3,128]{4,3,1,0,2:T(4,128)(2,1)S(1)}, bf16[1,4,1,3,128]{4,3,1,0,2:T(4,128)(2,1)S(1)}, u32[]{:S(2)}, u32[]{:S(2)}) collective-permute-start(bf16[1,4,1,3,128]{4,3,1,0,2:T(4,128)(2,1)S(1)} %copy.72), channel_id=1, source_target_pairs={{8,0},{16,8},{24,16},{0,24},{9,1},{17,9},{25,17},{1,25},{10,2},{18... | collective-permute-start | bytes 9224 | tf_op jit(solution)/shard_map/ppermute | solution.py:33
  29.4 16.8 %copy-start.5 = (bf16[2,4,1,3,128]{4,1,3,2,0:T(4,128)(2,1)S(1)}, bf16[2,4,1,3,128]{4,1,3,2,0:T(4,128)(2,1)}, u32[]{:S(2)}) copy-start(bf16[2,4,1,3,128]{4,1,3,2,0:T(4,128)(2,1)} %param.11) | copy-start | bytes 18436
  29.4 20.3 %copy-start.6 = (f32[2,4,1,128]{3,2,1,0:T(1,128)S(1)}, f32[2,4,1,128]{3,2,1,0:T(1,128)}, u32[]{:S(2)}) copy-start(f32[2,4,1,128]{3,2,1,0:T(1,128)} %get-tuple-element.19) | copy-start | bytes 12292
  30.4 10.8 %collective-permute-start.2 = (bf16[4,1,1,128,256]{4,3,2,1,0:T(8,128)(2,1)S(1)}, bf16[4,1,1,128,256]{4,3,2,1,0:T(8,128)(2,1)S(1)}, u32[]{:S(2)}, u32[]{:S(2)}) collective-permute-start(bf16[4,1,1,128,256]{4,3,2,1,0:T(8,128)(2,1)S(1)} %get-tuple-element.9), channel_id=1, source_target_pairs={{0,2},{2,4},{4,6},{6,0},{1,3},{3,5},{5,7},{7,1},{8,10},{10,12},{12... | collective-permute-start | bytes 786440 | tf_op jit(solution)/shard_map/ppermute | solution.py:33
  32.1 13.7 %collective-permute-start.3 = (bf16[4,1,1,128,256]{4,3,2,1,0:T(8,128)(2,1)S(1)}, bf16[4,1,1,128,256]{4,3,2,1,0:T(8,128)(2,1)S(1)}, u32[]{:S(2)}, u32[]{:S(2)}) collective-permute-start(bf16[4,1,1,128,256]{4,3,2,1,0:T(8,128)(2,1)S(1)} %get-tuple-element.10), channel_id=1, source_target_pairs={{2,0},{4,2},{6,4},{0,6},{3,1},{5,3},{7,5},{1,7},{10,8},{12,10},{14... | collective-permute-start | bytes 786440 | tf_op jit(solution)/shard_map/ppermute | solution.py:33
  34.0 128.7 %copy-start.3 = (bf16[256,256]{1,0:T(8,128)(2,1)S(1)}, bf16[256,256]{1,0:T(8,128)(2,1)}, u32[]{:S(2)}) copy-start(bf16[256,256]{1,0:T(8,128)(2,1)} %param.17) | copy-start | bytes 393220
  46.0 157.2 %collective-permute-start.4 = (bf16[4,6,1,128,256]{4,3,2,1,0:T(8,128)(2,1)S(1)}, bf16[4,6,1,128,256]{4,3,2,1,0:T(8,128)(2,1)}, u32[]{:S(2)}, u32[]{:S(2)}) collective-permute-start(bf16[4,6,1,128,256]{4,3,2,1,0:T(8,128)(2,1)S(1)} %pad_maximum_fusion), channel_id=1, source_target_pairs={{0,1},{1,0},{2,3},{3,2},{4,5},{5,4},{6,7},{7,6},{8,9},{9,8},{10,11... | collective-permute-start | bytes 4718600 | tf_op jit(solution)/shard_map/ppermute | solution.py:206
  46.8 10.7 %collective-permute-start.7 = (bf16[4,1,1,3,128]{4,3,1,0,2:T(4,128)(2,1)}, bf16[4,1,1,3,128]{4,3,1,0,2:T(4,128)(2,1)}, u32[]{:S(2)}, u32[]{:S(2)}) collective-permute-start(bf16[4,1,1,3,128]{4,3,1,0,2:T(4,128)(2,1)} %get-tuple-element.13), channel_id=1, source_target_pairs={{0,2},{2,4},{4,6},{6,0},{1,3},{3,5},{5,7},{7,1},{8,10},{10,12},{12... | collective-permute-start | bytes 9224 | tf_op jit(solution)/shard_map/ppermute | solution.py:33
  48.2 9.2 %collective-permute-start.8 = (bf16[4,1,1,3,128]{4,3,1,0,2:T(4,128)(2,1)}, bf16[4,1,1,3,128]{4,3,1,0,2:T(4,128)(2,1)}, u32[]{:S(2)}, u32[]{:S(2)}) collective-permute-start(bf16[4,1,1,3,128]{4,3,1,0,2:T(4,128)(2,1)} %get-tuple-element.14), channel_id=1, source_target_pairs={{2,0},{4,2},{6,4},{0,6},{3,1},{5,3},{7,5},{1,7},{10,8},{12,10},{14... | collective-permute-start | bytes 9224 | tf_op jit(solution)/shard_map/ppermute | solution.py:33
  58.1 1.3 collective-permute-start.9
Sparse Core Ops, SparseCore 0:
  25.0 136.6 reduce-scatter.1

commit v2 on v1

--- a/solution.py
+++ b/solution.py
@@ -67,19 +67,7 @@
                     dz = nz - hb[2, p0 : p0 + chunk]
                     if fold_z and oz == 1:
                         dz = 1.0 - jnp.abs(dz)
-                    sq = jnp.minimum(dx * dx + dy * dy + dz * dz, 1.0)
-                    dist = sq * lax.rsqrt(jnp.maximum(sq, 1e-30))
-                    ratio = jnp.exp2(dist * (2.0 * sharpness / (levels - 1) * math.log2(math.e)))
-                    edge = 1.0 - sq
-                    val = edge * edge * jnp.exp2(sq * (-sharpness * math.log2(math.e)))
-                    if center:
-                        row = lax.broadcasted_iota(jnp.int32, val.shape, 0) + p0
-                        lane = lax.broadcasted_iota(jnp.int32, val.shape, 1)
-                        val = jnp.where(row == lane, 0.0, val)
-                    for b in range(levels):
-                        phi[ox, b * slots + p0 : b * slots + p0 + chunk, col : col + slots] = val.astype(jnp.bfloat16)
-                        if b + 1 < levels:
-                            val = val * ratio
+                    radial_terms(dx, dy, dz, levels, center, p0, phi.at[ox], col, slots)
         rows = feat_ref[x + ox, z, pl.ds(y, 3)].reshape(3 * near_z * slots, feat)
         part = jnp.dot(phi[ox], rows, preferred_element_type=jnp.float32)
         if ox == 0:
@@ -126,6 +114,233 @@
     hidden = (joined / (1.0 + jnp.exp(-joined))).astype(jnp.bfloat16)
     result = feat_ref[0].astype(jnp.float32) + jnp.dot(hidden, wo_ref[...], preferred_element_type=jnp.float32)
     out_ref[0] = (result * home_ref[0, :, 3:4]).astype(jnp.bfloat16)
+
+
+def coords(index, counts):
+    return (index // (counts[1] * counts[2]), (index // counts[2]) % counts[1], index % counts[2])
+
+
+def layer_kernel(
+    counts,
+    levels,
+    pack_ref,
+    home_ref,
+    pos_ref,
+    wave_ref,
+    wb_ref,
+    damp_ref,
+    mix_ref,
+    we_ref,
+    wm_ref,
+    wo_ref,
+    out_ref,
+    wide,
+    hb,
+    phi,
+    acc,
+    basis,
+    struct,
+    parts,
+    share,
+    field,
+    msg,
+    halo_send,
+    halo_recv,
+    own_sem,
+    part_send,
+    part_recv,
+    share_send,
+    share_recv,
+):
+    cx, cy = pack_ref.shape[0], pack_ref.shape[1]
+    cells, slots, feat = out_ref.shape
+    waves = wave_ref.shape[0]
+    devices = counts[0] * counts[1] * counts[2]
+    rows = waves // devices
+    at = (lax.axis_index("gx"), lax.axis_index("gy"), lax.axis_index("gz"))
+    me = (at[0] * counts[1] + at[1]) * counts[2] + at[2]
+    mesh_id = pl.DeviceIdType.MESH
+
+    barrier = pltpu.get_barrier_semaphore()
+
+    @pl.loop(1, devices)
+    def _(k):
+        pl.semaphore_signal(barrier, inc=1, device_id=coords((me + k) % devices, counts), device_id_type=mesh_id)
+
+    pl.semaphore_wait(barrier, devices - 1)
+
+    own = pltpu.make_async_copy(pack_ref, wide.at[pl.ds(1, cx), pl.ds(1, cy), 0], own_sem)
+    own.start()
+
+    def span(step, length):
+        if step == 0:
+            return 0, 1, length
+        if step == 1:
+            return length - 1, 0, 1
+        return 0, length + 1, 1
+
+    halo = []
+    for dx in (1, -1, 0):
+        for dy in (1, -1, 0):
+            for dz in (0, 1):
+                if (dx, dy, dz) == (0, 0, 0):
+                    continue
+                sx, tx, lx = span(dx, cx)
+                sy, ty, ly = span(dy, cy)
+                target = (
+                    (at[0] + dx + counts[0]) % counts[0],
+                    (at[1] + dy + counts[1]) % counts[1],
+                    (at[2] + dz) % counts[2],
+                )
+                copy = pltpu.make_async_remote_copy(
+                    src_ref=pack_ref.at[pl.ds(sx, lx), pl.ds(sy, ly)],
+                    dst_ref=wide.at[pl.ds(tx, lx), pl.ds(ty, ly), dz],
+                    send_sem=halo_send.at[len(halo)],
+                    recv_sem=halo_recv.at[len(halo)],
+                    device_id=target,
+                    device_id_type=mesh_id,
+                )
+                copy.start()
+                halo.append(copy)
+
+    @pl.loop(0, cells)
+    def _(cell):
+        pos = pos_ref[cell]
+        lanes = pl.ds(pl.multiple_of(cell * slots, slots), slots)
+        chunk = 64
+        for w0 in range(0, waves, chunk):
+            wv = wave_ref[w0 : w0 + chunk]
+            turns = wv[:, 0:1] * pos[0:1] + wv[:, 1:2] * pos[1:2] + wv[:, 2:3] * pos[2:3]
+            u = turns - jnp.floor(turns + 0.5)
+            q = u * u
+            s = u * poly(q, SIN_C)
+            c = poly(q, COS_C)
+            basis[w0 : w0 + chunk, lanes] = (1.0 - 2.0 * s * s).astype(jnp.bfloat16)
+            basis[waves + w0 : waves + w0 + chunk, lanes] = (2.0 * s * c).astype(jnp.bfloat16)
+
+    atoms = pack_ref[:, :, 0:slots, :].reshape(cells * slots, feat)
+    struct[...] = (
+        jnp.dot(basis[...], atoms, preferred_element_type=jnp.float32)
+        .astype(jnp.bfloat16)
+        .reshape(2, devices, rows, feat)
+    )
+
+    def part_copy(k):
+        peer = (me + k) % devices
+        return pltpu.make_async_remote_copy(
+            src_ref=struct.at[:, peer],
+            dst_ref=parts.at[k],
+            send_sem=part_send.at[k],
+            recv_sem=part_recv.at[k],
+            device_id=coords(peer, counts),
+            device_id_type=mesh_id,
+        )
+
+    def share_copy(k, slot):
+        return pltpu.make_async_remote_copy(
+            src_ref=share,
+            dst_ref=field.at[:, slot],
+            send_sem=share_send.at[k],
+            recv_sem=share_recv.at[k],
+            device_id=coords((me + k) % devices, counts),
+            device_id_type=mesh_id,
+        )
+
+    @pl.loop(1, devices)
+    def _(k):
+        part_copy(k).start()
+
+    own.wait()
+    for copy in halo:
+        copy.wait()
+
+    @pl.loop(0, cells)
+    def _(cell):
+        @pl.when(cell == cells // 2)
+        def _():
+            @pl.loop(1, devices)
+            def _(k):
+                part_copy(k).wait()
+
+            parts[0] = struct[:, me]
+            total = jnp.sum(parts[...].astype(jnp.float32), axis=0).reshape(2 * rows, feat)
+            mixed = jnp.dot(total, mix_ref[...], precision=lax.Precision.HIGHEST, preferred_element_type=jnp.float32)
+            filtered = (mixed * damp_ref[...]).astype(jnp.bfloat16)
+            projected = jnp.dot(filtered, we_ref[...], preferred_element_type=jnp.float32)
+            projected = projected.astype(jnp.bfloat16).reshape(2, rows, feat)
+            share[...] = projected
+            field[:, me] = projected
+
+            @pl.loop(1, devices)
+            def _(k):
+                share_copy(k, me).start()
+
+        x = cell // cy
+        y = cell % cy
+        for a in range(3):
+            hb[a] = jnp.broadcast_to(home_ref[cell, :, a : a + 1], (slots, slots))
+        chunk = 32
+        for ox in range(3):
+            for oy in range(3):
+                for oz in range(2):
+                    g = wide[x + ox, y + oy, oz, slots : slots + 16, 0:slots].astype(jnp.float32)
+                    nx = g[0:1] + (ox - 1.0)
+                    ny = g[1:2] + (oy - 1.0)
+                    nz = g[2:3]
+                    col = (oy * 2 + oz) * slots
+                    for p0 in range(0, slots, chunk):
+                        gx = nx - hb[0, p0 : p0 + chunk]
+                        gy = ny - hb[1, p0 : p0 + chunk]
+                        gz = nz - hb[2, p0 : p0 + chunk]
+                        if oz == 1:
+                            gz = 1.0 - jnp.abs(gz)
+                        radial_terms(gx, gy, gz, levels, (ox, oy, oz) == (1, 1, 0), p0, phi.at[ox], col, slots)
+            near = wide[x + ox, pl.ds(y, 3), :, 0:slots].reshape(6 * slots, feat)
+            part = jnp.dot(phi[ox], near, preferred_element_type=jnp.float32)
+            if ox == 0:
+                acc[...] = part
+            elif ox == 1:
+                acc[...] += part
+        total = jnp.zeros((slots, feat), jnp.float32)
+        for b in range(levels):
+            both = acc[b * slots : (b + 1) * slots] + part[b * slots : (b + 1) * slots]
+            total = total + both * wb_ref[b : b + 1]
+        msg[cell] = total.astype(jnp.bfloat16)
+
+    @pl.loop(1, devices)
+    def _(k):
+        share_copy(k, (me - k + devices) % devices).wait()
+
+    waves_field = field[...].reshape(2 * waves, feat)
+
+    @pl.loop(0, cells)
+    def _(cell):
+        lanes = pl.ds(pl.multiple_of(cell * slots, slots), slots)
+        far = lax.dot_general(
+            basis[:, lanes], waves_field, (((0,), (0,)), ((), ())), preferred_element_type=jnp.float32
+        )
+        joined = far + jnp.dot(msg[cell], wm_ref[...], preferred_element_type=jnp.float32)
+        hidden = (joined / (1.0 + jnp.exp(-joined))).astype(jnp.bfloat16)
+        atom = pack_ref[cell // cy, cell % cy, 0:slots].astype(jnp.float32)
+        result = atom + jnp.dot(hidden, wo_ref[...], preferred_element_type=jnp.float32)
+        out_ref[cell] = (result * home_ref[cell, :, 3:4]).astype(jnp.bfloat16)
+
+
+def radial_terms(gx, gy, gz, levels, center, p0, phi, col, slots):
+    rows = gx.shape[0]
+    sq = jnp.minimum(gx * gx + gy * gy + gz * gz, 1.0)
+    dist = sq * lax.rsqrt(jnp.maximum(sq, 1e-30))
+    ratio = jnp.exp2(dist * (2.0 * sharpness / (levels - 1) * math.log2(math.e)))
+    edge = 1.0 - sq
+    val = edge * edge * jnp.exp2(sq * (-sharpness * math.log2(math.e)))
+    if center:
+        row = lax.broadcasted_iota(jnp.int32, val.shape, 0) + p0
+        lane = lax.broadcasted_iota(jnp.int32, val.shape, 1)
+        val = jnp.where(row == lane, 0.0, val)
+    for b in range(levels):
+        phi[b * slots + p0 : b * slots + p0 + rows, col : col + slots] = val.astype(jnp.bfloat16)
+        if b + 1 < levels:
+            val = val * ratio
 
 
 def body(
@@ -173,6 +388,50 @@
     )
     wave_turn = (index / lengths[:, None]).T
 
+    fold_z = grid[2] == 2 and cz == 1
+    level = jnp.arange(levels, dtype=jnp.float32) / (levels - 1)
+    wb = radial_weight * (jnp.exp(-sharpness * level * level) / math.sqrt(4.0 * slots))[:, None]
+    wb = jnp.repeat(wb, feat // heads, axis=1)
+    counts = tuple(lax.axis_size(n) for n in axes)
+    rows = waves // devices
+    if fold_z and rows % 16 == 0 and min(counts) > 1:
+        spread = jnp.pad(fractions, ((0, 0),) * 3 + ((0, 13), (0, feat - slots)))
+        pack = jnp.concatenate([masked, spread], axis=3).reshape(cx, cy, slots + 16, feat)
+        damp = lax.dynamic_slice_in_dim(damping, lax.axis_index(axes) * rows, rows, 0)
+        damp = jnp.concatenate([damp, damp]).reshape(2 * rows, 1)
+        vmem = pl.BlockSpec(memory_space=pltpu.VMEM)
+        dma = pltpu.SemaphoreType.DMA
+        out = pl.pallas_call(
+            functools.partial(layer_kernel, counts, levels),
+            in_specs=[vmem] * 10,
+            out_specs=vmem,
+            out_shape=jax.ShapeDtypeStruct((cells, slots, feat), jnp.bfloat16),
+            scratch_shapes=[
+                pltpu.VMEM((cx + 2, cy + 2, 2, slots + 16, feat), jnp.bfloat16),
+                pltpu.VMEM((3, slots, slots), jnp.float32),
+                pltpu.VMEM((3, levels * slots, 6 * slots), jnp.bfloat16),
+                pltpu.VMEM((levels * slots, feat), jnp.float32),
+                pltpu.VMEM((2 * waves, cells * slots), jnp.bfloat16),
+                pltpu.VMEM((2, devices, rows, feat), jnp.bfloat16),
+                pltpu.VMEM((devices, 2, rows, feat), jnp.bfloat16),
+                pltpu.VMEM((2, rows, feat), jnp.bfloat16),
+                pltpu.VMEM((2, devices, rows, feat), jnp.bfloat16),
+                pltpu.VMEM((cells, slots, feat), jnp.bfloat16),
+                dma((17,)),
+                dma((17,)),
+                dma,
+                dma((devices,)),
+                dma((devices,)),
+                dma((devices,)),
+                dma((devices,)),
+            ],
+            compiler_params=pltpu.CompilerParams(
+                collective_id=0, has_side_effects=True, vmem_limit_bytes=56 * 2**20
+            ),
+            name="layer",
+        )(pack, home, pos, wave_turn, wb, damp, ewald_mix, ewald_weight, msg_weight, out_weight)
+        return out.reshape(features.shape)
+
     basis, struct = pl.pallas_call(
         basis_kernel,
         grid=(cells,),
@@ -198,7 +457,6 @@
     projected = jnp.dot(filtered, ewald_weight, preferred_element_type=jnp.float32).astype(jnp.bfloat16)
     field = lax.all_gather(projected, axes, axis=1, tiled=True).reshape(2 * waves, feat)
 
-    fold_z = grid[2] == 2 and cz == 1
     wide_feat = widen(widen(masked, "gx", 0), "gy", 1)
     wide_geom = widen(widen(fractions, "gx", 0), "gy", 1)
     if fold_z:
@@ -212,9 +470,6 @@
         near_z = 3
     wide_feat = jnp.stack([wide_feat[:, :, z : z + near_z] for z in range(cz)], axis=1)
     wide_geom = jnp.stack([wide_geom[:, :, z : z + near_z] for z in range(cz)], axis=1).astype(jnp.float32)
-    level = jnp.arange(levels, dtype=jnp.float32) / (levels - 1)
-    wb = radial_weight * (jnp.exp(-sharpness * level * level) / math.sqrt(4.0 * slots))[:, None]
-    wb = jnp.repeat(wb, feat // heads, axis=1)
     messages = pl.pallas_call(
         functools.partial(message_kernel, cy, cz, fold_z, levels),
         grid=(cells,),

time: 241 us -> 87.4 us (0.36)
  the two profiles are of different devices: /device:TPU:0 before, /device:TPU:29 now
where the time goes in v2:
time: 87.4 us; the launch traced here: 87.1 us
  Pallas kernels  76.3 us (87%)
  local copies, waits for them, and re-layouts  6.14 us (7%)
  other arithmetic  4.6 us (5%)
    pallas_call x1, Pallas kernels, body(): pl.pallas_call(functools.partial(layer_kernel, counts, levels), in_specs=...  76.3 us
    unnamed x7, local copies, waits for them, and re-layouts  1.89 us

profile of v2, /device:TPU:29, one launch (start us, length us, event | category | flops | bytes accessed | tf_op | source)
XLA Modules:
  0.0 87.1 jit_solution(6410785941764668040)
XLA Ops:
  0.0 0.8 fusion.3
  0.8 0.0 copy-start
  0.8 0.1 dynamic_slice.3
  0.9 0.1 maximum_bitcast_fusion.1
  1.0 0.7 copy.61.damp_ref
  1.7 0.1 stack_broadcast_in_dim.9
  1.7 0.1 pad.9.clone
  1.8 0.1 maximum_bitcast_fusion
  1.9 0.8 broadcast_add_fusion
  2.7 0.6 copy.57
  3.3 0.8 fusion.8
  4.0 1.2 %bitcast_multiply_fusion = bf16[2,4,1,128,256]{4,3,1,0,2:T(8,128)(2,1)S(1)} fusion(bf16[2,4,1,128,256]{4,3,2,1,0:T(8,128)(2,1)} %param.10, bf16[2,4,128]{2,1,0:T(4,128)(2,1)S(1)} %bitcast.26), kind=kLoop, calls=%fused_computation.4 | loop fusion | flops 262144 | bytes 1050624 | tf_op jit(solution)/shard_map/mul | solution.py:367
  5.3 0.0 copy-done
  5.3 0.8 fusion.2.pack_ref
  6.2 0.0 copy-start.1
  6.2 1.0 %copy.55 = f32[8,4,128]{1,2,0:T(8,128)} copy(f32[8,4,128]{2,0,1:T(8,128)S(1)} %pad_maximum_fusion) | data formatting | bytes 32768 | tf_op jit(solution)/shard_map/concatenate | solution.py:370
  7.2 0.8 copy.58
  8.1 0.0 copy-done.1
  8.1 0.1 copy.59
  8.2 0.1 broadcast_in_dim.2
  8.2 0.7 reshape.60.wb_ref
  8.9 76.3 %layer.1 = bf16[8,128,256]{2,1,0:T(8,128)(2,1)} custom-call(bf16[2,4,144,256]{3,2,1,0:T(8,128)(2,1)} %fusion.2.pack_ref, f32[8,128,4]{2,1,0:T(8,128)} %bitcast.20, f32[8,3,128]{2,1,0:T(4,128)} %bitcast.23, f32[512,3]{1,0:T(8,128)} %bitcast.22, f32[8,256]{1,0:T(8,128)} %reshape.60.wb_ref, f32[32,1]{1,0:T(8,128)} %copy.61.damp_ref, f32[256,256]{1,0:T(8,128)} %mix_ref.1, ...), custom_call_target="tpu_custom_call" | custom-call | tf_op jit(solution)/shard_map/layer/pallas_call | solution.py:404
  85.2 1.9 %copy.68 = bf16[2,4,1,128,256]{4,3,2,1,0:T(8,128)(2,1)} copy(bf16[2,4,1,128,256]{4,3,2,1,0:T(8,128)(2,1)} %bitcast.21) | data formatting | bytes 1048576
  (11 shorter events, 0.1 us)
Async XLA Ops:
  0.8 4.5 %copy-start = (bf16[2,4,1,3,128]{4,1,3,2,0:T(4,128)(2,1)S(1)}, bf16[2,4,1,3,128]{4,1,3,2,0:T(4,128)(2,1)}, u32[]{:S(2)}) copy-start(bf16[2,4,1,3,128]{4,1,3,2,0:T(4,128)(2,1)} %param.11) | copy-start | bytes 18436
  6.2 1.9 %copy-start.1 = (f32[8,4]{0,1:T(4,128)S(1)}, f32[8,4]{0,1:T(4,128)}, u32[]{:S(2)}) copy-start(f32[8,4]{0,1:T(4,128)} %param.14) | copy-start | bytes 388

commit v3 on v2

--- a/solution.py
+++ b/solution.py
@@ -140,13 +140,19 @@
     acc,
     basis,
     struct,
+    pair,
+    chip_sum,
     parts,
     share,
     field,
     msg,
     halo_send,
     halo_recv,
+    side_send,
+    side_recv,
     own_sem,
+    pair_send,
+    pair_recv,
     part_send,
     part_recv,
     share_send,
@@ -158,16 +164,30 @@
     devices = counts[0] * counts[1] * counts[2]
     rows = waves // devices
     at = (lax.axis_index("gx"), lax.axis_index("gy"), lax.axis_index("gz"))
-    me = (at[0] * counts[1] + at[1]) * counts[2] + at[2]
+    chips = counts[0] * counts[1]
+    chip = at[0] * counts[1] + at[1]
+    core = at[2]
     mesh_id = pl.DeviceIdType.MESH
 
+    partner = (at[0], at[1], 1 - core)
+
+    def same_core(k):
+        peer = (chip + k) % chips
+        return (peer // counts[1], peer % counts[1], core)
+
+    def to_partner(src, dst, send, recv):
+        return pltpu.make_async_remote_copy(
+            src_ref=src, dst_ref=dst, send_sem=send, recv_sem=recv, device_id=partner, device_id_type=mesh_id
+        )
+
     barrier = pltpu.get_barrier_semaphore()
 
-    @pl.loop(1, devices)
+    @pl.loop(1, chips)
     def _(k):
-        pl.semaphore_signal(barrier, inc=1, device_id=coords((me + k) % devices, counts), device_id_type=mesh_id)
-
-    pl.semaphore_wait(barrier, devices - 1)
+        pl.semaphore_signal(barrier, inc=1, device_id=same_core(k), device_id_type=mesh_id)
+
+    pl.semaphore_signal(barrier, inc=1, device_id=partner, device_id_type=mesh_id)
+    pl.semaphore_wait(barrier, chips)
 
     own = pltpu.make_async_copy(pack_ref, wide.at[pl.ds(1, cx), pl.ds(1, cy), 0], own_sem)
     own.start()
@@ -179,29 +199,29 @@
             return length - 1, 0, 1
         return 0, length + 1, 1
 
-    halo = []
+    halo, side = [], []
     for dx in (1, -1, 0):
         for dy in (1, -1, 0):
-            for dz in (0, 1):
-                if (dx, dy, dz) == (0, 0, 0):
-                    continue
-                sx, tx, lx = span(dx, cx)
-                sy, ty, ly = span(dy, cy)
-                target = (
-                    (at[0] + dx + counts[0]) % counts[0],
-                    (at[1] + dy + counts[1]) % counts[1],
-                    (at[2] + dz) % counts[2],
-                )
-                copy = pltpu.make_async_remote_copy(
-                    src_ref=pack_ref.at[pl.ds(sx, lx), pl.ds(sy, ly)],
-                    dst_ref=wide.at[pl.ds(tx, lx), pl.ds(ty, ly), dz],
-                    send_sem=halo_send.at[len(halo)],
-                    recv_sem=halo_recv.at[len(halo)],
-                    device_id=target,
-                    device_id_type=mesh_id,
-                )
-                copy.start()
-                halo.append(copy)
+            n = len(halo)
+            sx, tx, lx = span(dx, cx)
+            sy, ty, ly = span(dy, cy)
+            region = (pl.ds(tx, lx), pl.ds(ty, ly))
+            if (dx, dy) == (0, 0):
+                side.append(to_partner(pack_ref, wide.at[(*region, 1)], side_send.at[n], side_recv.at[n]))
+                continue
+            target = ((at[0] + dx + counts[0]) % counts[0], (at[1] + dy + counts[1]) % counts[1], core)
+            copy = pltpu.make_async_remote_copy(
+                src_ref=pack_ref.at[pl.ds(sx, lx), pl.ds(sy, ly)],
+                dst_ref=wide.at[(*region, 0)],
+                send_sem=halo_send.at[n],
+                recv_sem=halo_recv.at[n],
+                device_id=target,
+                device_id_type=mesh_id,
+            )
+            copy.start()
+            halo.append(copy)
+            side.append(to_partner(wide.at[(*region, 0)], wide.at[(*region, 1)], side_send.at[n], side_recv.at[n]))
+    side[-1].start()
 
     @pl.loop(0, cells)
     def _(cell):
@@ -222,58 +242,78 @@
     struct[...] = (
         jnp.dot(basis[...], atoms, preferred_element_type=jnp.float32)
         .astype(jnp.bfloat16)
-        .reshape(2, devices, rows, feat)
+        .reshape(2, chips, 2, rows, feat)
     )
+    swap = to_partner(struct.at[:, :, 1 - core], pair, pair_send.at[0], pair_recv.at[0])
+    swap.start()
 
     def part_copy(k):
-        peer = (me + k) % devices
         return pltpu.make_async_remote_copy(
-            src_ref=struct.at[:, peer],
+            src_ref=chip_sum.at[:, (chip + k) % chips],
             dst_ref=parts.at[k],
             send_sem=part_send.at[k],
             recv_sem=part_recv.at[k],
-            device_id=coords(peer, counts),
+            device_id=same_core(k),
             device_id_type=mesh_id,
         )
 
     def share_copy(k, slot):
         return pltpu.make_async_remote_copy(
             src_ref=share,
-            dst_ref=field.at[:, slot],
+            dst_ref=field.at[:, slot, core],
             send_sem=share_send.at[k],
             recv_sem=share_recv.at[k],
-            device_id=coords((me + k) % devices, counts),
+            device_id=same_core(k),
             device_id_type=mesh_id,
         )
 
-    @pl.loop(1, devices)
+    def field_copy(half):
+        mine = field.at[:, :, half]
+        return to_partner(mine, mine, pair_send.at[1], pair_recv.at[1])
+
+    swap.wait()
+    both = struct[:, :, core].astype(jnp.float32) + pair[...].astype(jnp.float32)
+    chip_sum[...] = both.astype(jnp.bfloat16)
+
+    @pl.loop(1, chips)
     def _(k):
         part_copy(k).start()
 
     own.wait()
-    for copy in halo:
+    for n, copy in enumerate(halo):
+        copy.wait()
+        side[n].start()
+    for copy in side:
         copy.wait()
 
     @pl.loop(0, cells)
     def _(cell):
-        @pl.when(cell == cells // 2)
+        @pl.when(cell == cells // 4)
         def _():
-            @pl.loop(1, devices)
+            @pl.loop(1, chips)
             def _(k):
                 part_copy(k).wait()
 
-            parts[0] = struct[:, me]
+            parts[0] = chip_sum[:, chip]
             total = jnp.sum(parts[...].astype(jnp.float32), axis=0).reshape(2 * rows, feat)
             mixed = jnp.dot(total, mix_ref[...], precision=lax.Precision.HIGHEST, preferred_element_type=jnp.float32)
             filtered = (mixed * damp_ref[...]).astype(jnp.bfloat16)
             projected = jnp.dot(filtered, we_ref[...], preferred_element_type=jnp.float32)
             projected = projected.astype(jnp.bfloat16).reshape(2, rows, feat)
             share[...] = projected
-            field[:, me] = projected
-
-            @pl.loop(1, devices)
+            field[:, chip, core] = projected
+
+            @pl.loop(1, chips)
             def _(k):
-                share_copy(k, me).start()
+                share_copy(k, chip).start()
+
+        @pl.when(cell == cells - 1)
+        def _():
+            @pl.loop(1, chips)
+            def _(k):
+                share_copy(k, (chip - k + chips) % chips).wait()
+
+            field_copy(core).start()
 
         x = cell // cy
         y = cell % cy
@@ -307,9 +347,8 @@
             total = total + both * wb_ref[b : b + 1]
         msg[cell] = total.astype(jnp.bfloat16)
 
-    @pl.loop(1, devices)
-    def _(k):
-        share_copy(k, (me - k + devices) % devices).wait()
+    field_copy(core).wait_send()
+    field_copy(1 - core).wait_recv()
 
     waves_field = field[...].reshape(2 * waves, feat)
 
@@ -394,6 +433,7 @@
     wb = jnp.repeat(wb, feat // heads, axis=1)
     counts = tuple(lax.axis_size(n) for n in axes)
     rows = waves // devices
+    chips = counts[0] * counts[1]
     if fold_z and rows % 16 == 0 and min(counts) > 1:
         spread = jnp.pad(fractions, ((0, 0),) * 3 + ((0, 13), (0, feat - slots)))
         pack = jnp.concatenate([masked, spread], axis=3).reshape(cx, cy, slots + 16, feat)
@@ -412,18 +452,24 @@
                 pltpu.VMEM((3, levels * slots, 6 * slots), jnp.bfloat16),
                 pltpu.VMEM((levels * slots, feat), jnp.float32),
                 pltpu.VMEM((2 * waves, cells * slots), jnp.bfloat16),
-                pltpu.VMEM((2, devices, rows, feat), jnp.bfloat16),
-                pltpu.VMEM((devices, 2, rows, feat), jnp.bfloat16),
+                pltpu.VMEM((2, chips, 2, rows, feat), jnp.bfloat16),
+                pltpu.VMEM((2, chips, rows, feat), jnp.bfloat16),
+                pltpu.VMEM((2, chips, rows, feat), jnp.bfloat16),
+                pltpu.VMEM((chips, 2, rows, feat), jnp.bfloat16),
                 pltpu.VMEM((2, rows, feat), jnp.bfloat16),
-                pltpu.VMEM((2, devices, rows, feat), jnp.bfloat16),
+                pltpu.VMEM((2, chips, 2, rows, feat), jnp.bfloat16),
                 pltpu.VMEM((cells, slots, feat), jnp.bfloat16),
-                dma((17,)),
-                dma((17,)),
+                dma((8,)),
+                dma((8,)),
+                dma((9,)),
+                dma((9,)),
                 dma,
-                dma((devices,)),
-                dma((devices,)),
-                dma((devices,)),
-                dma((devices,)),
+                dma((2,)),
+                dma((2,)),
+                dma((chips,)),
+                dma((chips,)),
+                dma((chips,)),
+                dma((chips,)),
             ],
             compiler_params=pltpu.CompilerParams(
                 collective_id=0, has_side_effects=True, vmem_limit_bytes=56 * 2**20

time: 87.4 us -> 64.8 us (0.74)
  the two profiles are of different devices: /device:TPU:29 before, /device:TPU:0 now
where the time goes in v3:
time: 64.8 us; the launch traced here: 64.5 us
  Pallas kernels  53.7 us (83%)
  local copies, waits for them, and re-layouts  6.14 us (9%)
  other arithmetic  4.6 us (7%)
    pallas_call x1, Pallas kernels, body(): pl.pallas_call(functools.partial(layer_kernel, counts, levels), in_specs=...  53.7 us
    unnamed x7, local copies, waits for them, and re-layouts  1.89 us

profile of v3, /device:TPU:0, one launch (start us, length us, event | category | flops | bytes accessed | tf_op | source)
XLA Modules:
  0.0 64.5 jit_solution(3025217919980628582)
XLA Ops:
  0.0 0.8 %fusion.3 = (f32[512]{0:T(512)S(1)}, f32[3,512]{1,0:T(4,128)S(1)}) fusion(s32[3,512]{1,0:T(4,128)} %param.13, f32[3]{0:T(128)} %constant.54), kind=kLoop, calls=%fused_computation.7 | loop fusion | flops 8704 | bytes 14348 | tf_op jit(solution)/shard_map/reduce_sum | solution.py:421
  0.8 0.0 copy-start
  0.8 0.1 dynamic_slice.3
  0.9 0.1 maximum_bitcast_fusion.1
  1.0 0.7 %copy.61.damp_ref = f32[32,1]{1,0:T(8,128)} copy(f32[32,1]{0,1:T(1,128)S(1)} %maximum_bitcast_fusion.1) | data formatting | bytes 256 | tf_op jit(solution)/shard_map/reshape | solution.py:441
  1.7 0.1 stack_broadcast_in_dim.9
  1.7 0.1 pad.9.clone
  1.8 0.1 maximum_bitcast_fusion
  1.9 0.8 %broadcast_add_fusion = f32[2,4,1,3,128]{4,1,3,2,0:T(4,128)S(1)} fusion(f32[2,4,3]{1,2,0:T(4,128)S(1)} %copy.56, bf16[2,4,1,3,128]{4,1,3,2,0:T(4,128)(2,1)} %param.11), kind=kLoop, calls=%fused_computation.9 | loop fusion | flops 6144 | bytes 18528 | tf_op jit(solution)/shard_map/add | solution.py:417
  2.7 0.6 copy.57
  3.3 0.8 %fusion.8 = (f32[2,4,1,128]{3,2,1,0:T(1,128)S(1)}, bf16[2,4,1,128]{3,2,1,0:T(2,128)(2,1)S(1)}) fusion(s32[2,4,1,128]{3,2,1,0:T(1,128)} %param.12), kind=kLoop, calls=%fused_computation.23 | loop fusion | flops 2048 | bytes 10240 | tf_op jit(solution)/shard_map/convert_element_type | solution.py:409
  4.0 1.2 %bitcast_multiply_fusion = bf16[2,4,1,128,256]{4,3,1,0,2:T(8,128)(2,1)S(1)} fusion(bf16[2,4,1,128,256]{4,3,2,1,0:T(8,128)(2,1)} %param.10, bf16[2,4,128]{2,1,0:T(4,128)(2,1)S(1)} %bitcast.26), kind=kLoop, calls=%fused_computation.4 | loop fusion | flops 262144 | bytes 1050624 | tf_op jit(solution)/shard_map/mul | solution.py:406
  5.3 0.0 copy-done
  5.3 0.8 %fusion.2.pack_ref = bf16[2,4,144,256]{3,2,1,0:T(8,128)(2,1)} fusion(bf16[2,4,1,3,128]{4,3,1,0,2:T(4,128)(2,1)S(1)} %copy.53, bf16[2,4,1,128,256]{4,3,1,0,2:T(8,128)(2,1)S(1)} %bitcast_multiply_fusion), kind=kLoop, calls=%fused_computation.3 | loop fusion | flops 1769472 | bytes 1120256 | tf_op jit(solution)/shard_map/reshape | solution.py:439
  6.2 0.0 copy-start.1
  6.2 1.0 %copy.55 = f32[8,4,128]{1,2,0:T(8,128)} copy(f32[8,4,128]{2,0,1:T(8,128)S(1)} %pad_maximum_fusion) | data formatting | bytes 32768 | tf_op jit(solution)/shard_map/concatenate | solution.py:409
  7.2 0.8 %copy.58 = f32[3,512]{0,1:T(8,128)} copy(f32[3,512]{1,0:T(4,128)S(1)} %get-tuple-element.6) | data formatting | bytes 12288 | tf_op jit(solution)/shard_map/div | solution.py:428
  8.1 0.0 copy-done.1
  8.1 0.1 copy.59
  8.2 0.1 broadcast_in_dim.2
  8.2 0.7 %reshape.60.wb_ref = f32[8,256]{1,0:T(8,128)} reshape(f32[8,4,64]{2,1,0:T(4,128)S(1)} %broadcast_in_dim.2) | data formatting | bytes 16384 | tf_op jit(solution)/shard_map/reshape | solution.py:433
  8.9 53.7 %layer.1 = bf16[8,128,256]{2,1,0:T(8,128)(2,1)} custom-call(bf16[2,4,144,256]{3,2,1,0:T(8,128)(2,1)} %fusion.2.pack_ref, f32[8,128,4]{2,1,0:T(8,128)} %bitcast.20, f32[8,3,128]{2,1,0:T(4,128)} %bitcast.23, f32[512,3]{1,0:T(8,128)} %bitcast.22, f32[8,256]{1,0:T(8,128)} %reshape.60.wb_ref, f32[32,1]{1,0:T(8,128)} %copy.61.damp_ref, f32[256,256]{1,0:T(8,128)} %mix_ref.1, ...), custom_call_target="tpu_custom_call" | custom-call | tf_op jit(solution)/shard_map/layer/pallas_call | solution.py:444
  62.6 1.9 %copy.68 = bf16[2,4,1,128,256]{4,3,2,1,0:T(8,128)(2,1)} copy(bf16[2,4,1,128,256]{4,3,2,1,0:T(8,128)(2,1)} %bitcast.21) | data formatting | bytes 1048576
  (11 shorter events, 0.1 us)
Async XLA Ops:
  0.8 4.5 %copy-start = (bf16[2,4,1,3,128]{4,1,3,2,0:T(4,128)(2,1)S(1)}, bf16[2,4,1,3,128]{4,1,3,2,0:T(4,128)(2,1)}, u32[]{:S(2)}) copy-start(bf16[2,4,1,3,128]{4,1,3,2,0:T(4,128)(2,1)} %param.11) | copy-start | bytes 18436
  6.2 1.9 %copy-start.1 = (f32[8,4]{0,1:T(4,128)S(1)}, f32[8,4]{0,1:T(4,128)}, u32[]{:S(2)}) copy-start(f32[8,4]{0,1:T(4,128)} %param.14) | copy-start | bytes 388

commit v4 on v3

--- a/solution.py
+++ b/solution.py
@@ -226,6 +226,7 @@
     @pl.loop(0, cells)
     def _(cell):
         pos = pos_ref[cell]
+        filled = pack_ref[cell // cy, cell % cy, slots : slots + 16, 0:slots].astype(jnp.float32)[3:4]
         lanes = pl.ds(pl.multiple_of(cell * slots, slots), slots)
         chunk = 64
         for w0 in range(0, waves, chunk):
@@ -235,8 +236,8 @@
             q = u * u
             s = u * poly(q, SIN_C)
             c = poly(q, COS_C)
-            basis[w0 : w0 + chunk, lanes] = (1.0 - 2.0 * s * s).astype(jnp.bfloat16)
-            basis[waves + w0 : waves + w0 + chunk, lanes] = (2.0 * s * c).astype(jnp.bfloat16)
+            basis[w0 : w0 + chunk, lanes] = (filled * (1.0 - 2.0 * s * s)).astype(jnp.bfloat16)
+            basis[waves + w0 : waves + w0 + chunk, lanes] = (filled * (2.0 * s * c)).astype(jnp.bfloat16)
 
     atoms = pack_ref[:, :, 0:slots, :].reshape(cells * slots, feat)
     struct[...] = (
@@ -334,7 +335,7 @@
                         gz = nz - hb[2, p0 : p0 + chunk]
                         if oz == 1:
                             gz = 1.0 - jnp.abs(gz)
-                        radial_terms(gx, gy, gz, levels, (ox, oy, oz) == (1, 1, 0), p0, phi.at[ox], col, slots)
+                        radial_terms(gx, gy, gz, levels, (ox, oy, oz) == (1, 1, 0), p0, phi.at[ox], col, slots, g[3:4])
             near = wide[x + ox, pl.ds(y, 3), :, 0:slots].reshape(6 * slots, feat)
             part = jnp.dot(phi[ox], near, preferred_element_type=jnp.float32)
             if ox == 0:
@@ -365,13 +366,15 @@
         out_ref[cell] = (result * home_ref[cell, :, 3:4]).astype(jnp.bfloat16)
 
 
-def radial_terms(gx, gy, gz, levels, center, p0, phi, col, slots):
+def radial_terms(gx, gy, gz, levels, center, p0, phi, col, slots, filled=None):
     rows = gx.shape[0]
     sq = jnp.minimum(gx * gx + gy * gy + gz * gz, 1.0)
     dist = sq * lax.rsqrt(jnp.maximum(sq, 1e-30))
     ratio = jnp.exp2(dist * (2.0 * sharpness / (levels - 1) * math.log2(math.e)))
     edge = 1.0 - sq
     val = edge * edge * jnp.exp2(sq * (-sharpness * math.log2(math.e)))
+    if filled is not None:
+        val = val * filled
     if center:
         row = lax.broadcasted_iota(jnp.int32, val.shape, 0) + p0
         lane = lax.broadcasted_iota(jnp.int32, val.shape, 1)
@@ -435,8 +438,9 @@
     rows = waves // devices
     chips = counts[0] * counts[1]
     if fold_z and rows % 16 == 0 and min(counts) > 1:
-        spread = jnp.pad(fractions, ((0, 0),) * 3 + ((0, 13), (0, feat - slots)))
-        pack = jnp.concatenate([masked, spread], axis=3).reshape(cx, cy, slots + 16, feat)
+        spread = jnp.concatenate([fractions, occupied[:, :, :, None, :].astype(jnp.bfloat16)], axis=3)
+        spread = jnp.pad(spread, ((0, 0),) * 3 + ((0, 12), (0, feat - slots)))
+        pack = jnp.concatenate([features, spread], axis=3).reshape(cx, cy, slots + 16, feat)
         damp = lax.dynamic_slice_in_dim(damping, lax.axis_index(axes) * rows, rows, 0)
         damp = jnp.concatenate([damp, damp]).reshape(2 * rows, 1)
         vmem = pl.BlockSpec(memory_space=pltpu.VMEM)

time: 64.8 us -> 66.1 us (1.020)
  local copies, waits for them, and re-layouts: 6.14 us -> 7.49 us
    mul x1 -> x0, other arithmetic: 1.24 us -> none  [body(): masked = features * occupied[..., None].astype(jnp.bfloat16)]
    convert_element_type x1, local copies, waits for them, and re-layouts: 0.01 us -> 0.69 us  [body(): frac = fractions.astype(jnp.float32)]
    mul x1, other arithmetic: 0.01 us -> 0.69 us  [body(): radial_weight * (jnp.exp(-sharpness * level * level) / math.sqrt(4.0 * sl...]
    unnamed x7 -> x4, local copies, waits for them, and re-layouts: 1.89 us -> 2.57 us
where the time goes in v4:
time: 66.1 us; the launch traced here: 65.7 us
  Pallas kernels  54.1 us (82%)
  local copies, waits for them, and re-layouts  7.49 us (11%)
  other arithmetic  4.06 us (6%)
    pallas_call x1, Pallas kernels, body(): pl.pallas_call(functools.partial(layer_kernel, counts, levels), in_specs=...  54.1 us
    unnamed x4, local copies, waits for them, and re-layouts  2.57 us

profile of v4, /device:TPU:0, one launch (start us, length us, event | category | flops | bytes accessed | tf_op | source)
XLA Modules:
  0.0 65.7 jit_solution(14054912370408477907)
XLA Ops:
  0.0 0.0 copy-start
  0.0 0.1 pad.9.clone
  0.1 0.1 stack_broadcast_in_dim.9
  0.2 0.1 maximum_bitcast_fusion.1
  0.3 0.7 %broadcast_multiply_fusion = f32[8,4]{0,1:T(4,128)S(1)} fusion(f32[8,4]{0,1:T(4,128)} %param.14, f32[8]{0:T(128)S(1)} %fusion.10), kind=kLoop, calls=%fused_computation.18 | loop fusion | flops 32 | bytes 288 | tf_op jit(solution)/shard_map/mul | solution.py:435
  0.9 0.1 copy.63
  1.0 0.8 %broadcast_add_fusion = f32[2,4,1,3,128]{4,1,3,2,0:T(4,128)S(1)} fusion(f32[2,4,3]{1,2,0:T(4,128)S(1)} %copy.60, bf16[2,4,1,3,128]{4,1,3,2,0:T(4,128)(2,1)} %param.11), kind=kLoop, calls=%fused_computation.13 | loop fusion | flops 6144 | bytes 18528 | tf_op jit(solution)/shard_map/add | solution.py:420
  1.8 0.6 copy.61
  2.4 0.7 %copy.55 = bf16[2,4,1,3,128]{4,3,1,0,2:T(4,128)(2,1)S(1)} copy(bf16[2,4,1,3,128]{4,1,3,2,0:T(4,128)(2,1)} %param.11) | data formatting | bytes 12288 | tf_op args[1]
  3.1 0.8 %fusion.11 = (f32[2,4,1,128]{3,2,1,0:T(1,128)S(1)}, bf16[2,4,1,1,128]{4,3,1,0,2:T(2,128)(2,1)S(1)}) fusion(s32[2,4,1,128]{3,2,1,0:T(1,128)} %param.12), kind=kLoop, calls=%fused_computation.27 | loop fusion | flops 2048 | bytes 10240 | tf_op jit(solution)/shard_map/convert_element_type | solution.py:412
  3.9 0.8 %fusion.6 = (f32[512]{0:T(512)S(1)}, f32[3,512]{1,0:T(4,128)S(1)}) fusion(s32[3,512]{1,0:T(4,128)} %param.13, f32[3]{0:T(128)} %constant.54), kind=kLoop, calls=%fused_computation.11 | loop fusion | flops 8704 | bytes 14348 | tf_op jit(solution)/shard_map/reduce_sum | solution.py:424
  4.7 0.1 dynamic_slice.3
  4.7 0.1 maximum_bitcast_fusion.2
  4.8 0.1 broadcast_in_dim.2
  4.9 0.7 %reshape.63.wb_ref = f32[8,256]{1,0:T(8,128)} reshape(f32[8,4,64]{2,1,0:T(4,128)S(1)} %broadcast_in_dim.2) | data formatting | bytes 16384 | tf_op jit(solution)/shard_map/reshape | solution.py:436
  5.6 0.7 %copy.58 = f32[2,4,1,3,128]{4,1,0,3,2:T(4,128)S(1)} copy(bf16[2,4,1,3,128]{4,1,3,2,0:T(4,128)(2,1)} %param.11) | data formatting | bytes 18432 | tf_op jit(solution)/shard_map/convert_element_type | solution.py:410
  6.3 0.7 %copy.65.damp_ref = f32[32,1]{1,0:T(8,128)} copy(f32[32,1]{0,1:T(1,128)S(1)} %maximum_bitcast_fusion.2) | data formatting | bytes 256 | tf_op jit(solution)/shard_map/reshape | solution.py:445
  7.0 0.9 %copy.62 = f32[3,512]{0,1:T(8,128)} copy(f32[3,512]{1,0:T(4,128)S(1)} %get-tuple-element.6) | data formatting | bytes 12288 | tf_op jit(solution)/shard_map/div | solution.py:431
  7.8 1.0 %copy.59 = f32[8,4,128]{1,2,0:T(8,128)} copy(f32[8,4,128]{2,0,1:T(8,128)S(1)} %pad_maximum_fusion) | data formatting | bytes 32768 | tf_op jit(solution)/shard_map/concatenate | solution.py:412
  8.9 0.0 copy-done
  8.9 0.9 %maximum_bitcast_fusion.pack_ref = bf16[2,4,144,256]{3,2,1,0:T(8,128)(2,1)} fusion(bf16[2,4,1,16,256]{4,3,1,0,2:T(8,128)(2,1)S(1)} %fusion.5, bf16[2,4,1,128,256]{4,3,1,0,2:T(8,128)(2,1)S(1)} %bitcast.21), kind=kLoop, calls=%fused_computation | loop fusion | flops 1179648 | bytes 1179648 | tf_op jit(solution)/shard_map/reshape | solution.py:443
  9.7 54.1 %layer.1 = bf16[8,128,256]{2,1,0:T(8,128)(2,1)} custom-call(bf16[2,4,144,256]{3,2,1,0:T(8,128)(2,1)} %maximum_bitcast_fusion.pack_ref, f32[8,128,4]{2,1,0:T(8,128)} %bitcast.18, f32[8,3,128]{2,1,0:T(4,128)} %bitcast.22, f32[512,3]{1,0:T(8,128)} %bitcast.20, f32[8,256]{1,0:T(8,128)} %reshape.63.wb_ref, f32[32,1]{1,0:T(8,128)} %copy.65.damp_ref, ...), custom_call_target="tpu_custom_call" | custom-call | tf_op jit(solution)/shard_map/layer/pallas_call | solution.py:448
  63.9 1.9 %copy.69 = bf16[2,4,1,128,256]{4,3,2,1,0:T(8,128)(2,1)} copy(bf16[2,4,1,128,256]{4,3,2,1,0:T(8,128)(2,1)} %bitcast.19) | data formatting | bytes 1048576
  (8 shorter events, 0.1 us)
Async XLA Ops:
  0.0 8.9 %copy-start = (bf16[2,4,1,128,256]{4,3,2,1,0:T(8,128)(2,1)S(1)}, bf16[2,4,1,128,256]{4,3,2,1,0:T(8,128)(2,1)}, u32[]{:S(2)}) copy-start(bf16[2,4,1,128,256]{4,3,2,1,0:T(8,128)(2,1)} %param.10) | copy-start | bytes 1572868
